TPU v7x, 32 devices: a whole 2x2x4 slice. The times are simulated.
32 devices in a mesh: lon: 8 (over y, x, core), bal: 4 (over z).
Axes of the slice: x: 2, y: 2, z: 4, core: 2. Of those that a mesh axis runs over, the one named last changes fastest.
Arguments:
- conc: float32 [65536, 128], P(('lon', 'bal')), may hold values from -6 to 6
- neighbours: int32 [512, 8], P(('lon', 'bal')), may hold values from 0 to 511, as said below
- counts: int32 [512], P(('lon', 'bal')), may hold values from 1 to 8
- weights: int32 [512, 8], P(('lon', 'bal')), may hold values from 1 to 15
- zones: int32 [65536], P(('lon', 'bal')), may hold values from 0 to 31
- owners: int32 [65536, 1], P(('lon', 'bal')), may hold values from 0 to 3; in each aligned block of 2048 rows (0 to 2047, 2048 to 4095, ...) at most 1024 rows name the same one
- rate_table: float32 [32, 128], replicated, may hold values from 0.05 to 1
- reaction: bfloat16 [128, 128], replicated, may hold values from -0.5 to 0.5
Outputs:
- conc_out: bfloat16 [65536, 128], P(('lon', 'bal'))
- chem_slots: bfloat16 [131072, 128], P(('lon', 'bal'))
Inputs may be any that keep to these rules, and one draw needn't show every extreme that they name: neighbours[g, k] is a block of the same bal index as g, on the same longitude band or on the band just before or after it, with the bands wrapping around. On every trajectory owner, at most 1024 of its parcels have the same owners value; on some trajectory owners one value is taken exactly 1024 times.
All inputs are finite; a program needn't handle non-finite values.
Results may differ from a plain program's by a relative error of at most 0.0085.
Values may be sent and summed in bfloat16 or wider, within the bound.
No kernel may reach another device: no remote copies, remote signals or barrier semaphores. Data moves between devices by JAX's collectives and lax.ppermute only.
A program may use at most 64 MiB of HBM per device.

v0:
```python
import jax
import jax.numpy as jnp
from jax import lax
from jax.sharding import PartitionSpec as P

BLK = 128
KADJ = 8
ZONES = 32
SUBSTEPS = 12


def extended_2(cells, sides, width):
    for axis, dim in sides:
        count = lax.axis_size(axis)
        head = lax.slice_in_dim(cells, 0, width, axis=dim)
        tail = lax.slice_in_dim(cells, cells.shape[dim] - width, cells.shape[dim], axis=dim)
        cells = jnp.concatenate(
            [
                lax.ppermute(tail, axis, [(i, (i + 1) % count) for i in range(count)]),
                cells,
                lax.ppermute(head, axis, [((i + 1) % count, i) for i in range(count)]),
            ],
            axis=dim,
        )
    return cells


def shifted(value, axis, steps):
    count = lax.axis_size(axis)
    pairs = [(source, (source + steps) % count) for source in range(count)]
    return lax.ppermute(value, axis, pairs)


def chemistry(state, reaction):

    def advance(step_index, current):
        tendency = jnp.dot(
            current.astype(jnp.bfloat16), reaction, preferred_element_type=jnp.float32
        )
        return current + 0.25 * jnp.tanh(tendency)

    return lax.fori_loop(0, SUBSTEPS, advance, state.astype(jnp.float32)).astype(jnp.bfloat16)


def shards(conc, neighbours, counts, weights, zones, owners, rate_table, reaction):
    rows, width = conc.shape
    nblocks = rows // BLK
    lon_count = lax.axis_size("lon")
    bal_count = lax.axis_size("bal")
    device_count = lon_count * bal_count
    self_device = lax.axis_index("lon") * bal_count + lax.axis_index("bal")
    own_blocks = conc.reshape(nblocks, BLK, width)
    extended = extended_2(own_blocks, (("lon", 0),), nblocks)
    used = jnp.arange(KADJ, dtype=jnp.int32)[None, :] < counts[:, None]
    coefs = jnp.where(used, weights.astype(jnp.float32) / 128.0, 0.0)
    local_part = neighbours % nblocks
    apart = (neighbours // nblocks - self_device + device_count) % device_count
    ext_index = (
        jnp.where(apart == 0, nblocks, jnp.where(apart == bal_count, 2 * nblocks, 0)) + local_part
    )
    change = jnp.zeros((nblocks, BLK, width), jnp.float32)
    sent = jnp.zeros((3 * nblocks, BLK, width), jnp.float32)
    for column in range(KADJ):
        flux = coefs[:, column][:, None, None] * (extended[ext_index[:, column]] - own_blocks)
        change = change + flux
        sent = sent.at[ext_index[:, column]].add(flux)
    from_right = shifted(sent[:nblocks].astype(jnp.bfloat16), "lon", -1).astype(jnp.float32)
    from_left = shifted(sent[2 * nblocks :].astype(jnp.bfloat16), "lon", 1).astype(jnp.float32)
    change = change - sent[nblocks : 2 * nblocks] - from_right - from_left
    mixed = (own_blocks + change).reshape(rows, width)
    zone_table = (zones[:, None] == jnp.arange(ZONES, dtype=jnp.int32)[None, :]).astype(jnp.float32)
    rates = jnp.dot(zone_table, rate_table, precision=lax.Precision.HIGHEST)
    moved = (mixed * jnp.exp(-rates)).astype(jnp.bfloat16)
    capacity = 2 * rows // bal_count
    owner = owners[:, 0]
    owner_table = (owner[:, None] == jnp.arange(bal_count, dtype=jnp.int32)[None, :]).astype(
        jnp.int32
    )
    rank = jnp.sum((jnp.cumsum(owner_table, axis=0) - owner_table) * owner_table, axis=1)
    slot = owner * capacity + rank
    conc_out = chemistry(moved, reaction)
    outgoing = jnp.zeros((bal_count * capacity, width), jnp.bfloat16).at[slot].set(conc_out)
    outgoing = outgoing.reshape(bal_count, capacity, width)
    chem_slots = lax.all_to_all(outgoing, "bal", split_axis=0, concat_axis=0, tiled=True).reshape(
        -1, width
    )
    return (conc_out, chem_slots)


def solution(mesh):
    in_specs = (
        P(("lon", "bal"), None),
        P(("lon", "bal"), None),
        P(("lon", "bal")),
        P(("lon", "bal"), None),
        P(("lon", "bal")),
        P(("lon", "bal"), None),
        P(),
        P(),
    )
    out_specs = (P(("lon", "bal"), None), P(("lon", "bal"), None))
    return jax.shard_map(shards, mesh=mesh, in_specs=in_specs, out_specs=out_specs, check_vma=False)
```

profile of v0, /device:TPU:0, one launch (start us, length us, event | category | flops | bytes accessed | tf_op | source)
XLA Modules:
  0.0 134.0 jit_solution(15365341471317218973)
XLA Ops:
  0.6 0.5 collective-permute-start
  1.2 2.9 %collective-permute-start.1 = (f32[16,128,128]{2,1,0:T(8,128)}, f32[16,128,128]{2,1,0:T(8,128)}, u32[]{:S(2)}, u32[]{:S(2)}) collective-permute-start(f32[16,128,128]{2,1,0:T(8,128)} %bitcast.69), channel_id=1, source_target_pairs={{4,0},{8,4},{12,8},{16,12},{20,16},{24,20},{28,24},{0,28},{5,1},{9... | collective-permute-start | bytes 3145736 | tf_op jit(solution)/shard_map/ppermute | solution.py:21
  4.1 0.7 fusion.19
  4.9 0.7 fusion.15
  5.6 1.1 reduce-window.6
  7.1 0.7 multiply_select_fusion
  7.9 17.5 %collective-permute-done = f32[16,128,128]{2,1,0:T(8,128)S(1)} collective-permute-done((f32[16,128,128]{2,1,0:T(8,128)}, f32[16,128,128]{2,1,0:T(8,128)S(1)}, u32[]{:S(2)}, u32[]{:S(2)}) %collective-permute-start) | collective-permute-done | bytes 1048608 | tf_op jit(solution)/shard_map/ppermute | solution.py:19
  25.4 1.0 copy-done.7
  26.4 0.6 collective-permute-done.1
  27.0 2.1 %pad_maximum_fusion = f32[48,128,128]{2,1,0:T(8,128)S(1)} fusion(f32[16,128,128]{2,1,0:T(8,128)} %collective-permute-done.1, f32[16,128,128]{2,1,0:T(8,128)} %bitcast.70, f32[16,128,128]{2,1,0:T(8,128)} %copy-done.7), kind=kLoop, calls=%fused_computation.21 | loop fusion | flops 1572864 | bytes 6291456 | tf_op jit(solution)/shard_map/concatenate | solution.py:17
  29.0 1.6 %gather_fusion = f32[16,128,128]{2,1,0:T(8,128)} fusion(f32[48,128,128]{2,1,0:T(8,128)S(1)} %pad_maximum_fusion, s32[1024]{0:T(1024)S(1)} %get-tuple-element.59), kind=kCustom, calls=%fused_computation | custom fusion | bytes 2097216 | tf_op jit(solution)/shard_map/gather | solution.py:64
  30.6 1.6 %gather_fusion.1 = f32[16,128,128]{2,1,0:T(8,128)} fusion(f32[48,128,128]{2,1,0:T(8,128)S(1)} %pad_maximum_fusion, s32[1024]{0:T(1024)S(1)} %get-tuple-element.58), kind=kCustom, calls=%fused_computation.1 | custom fusion | bytes 2097216 | tf_op jit(solution)/shard_map/gather | solution.py:64
  32.3 1.6 %gather_fusion.2 = f32[16,128,128]{2,1,0:T(8,128)} fusion(f32[48,128,128]{2,1,0:T(8,128)S(1)} %pad_maximum_fusion, s32[1024]{0:T(1024)S(1)} %get-tuple-element.57), kind=kCustom, calls=%fused_computation.2 | custom fusion | bytes 2097216 | tf_op jit(solution)/shard_map/gather | solution.py:64
  33.9 1.6 %gather_fusion.3 = f32[16,128,128]{2,1,0:T(8,128)} fusion(f32[48,128,128]{2,1,0:T(8,128)S(1)} %pad_maximum_fusion, s32[1024]{0:T(1024)S(1)} %get-tuple-element.56), kind=kCustom, calls=%fused_computation.3 | custom fusion | bytes 2097216 | tf_op jit(solution)/shard_map/gather | solution.py:64
  35.5 1.6 %gather_fusion.4 = f32[16,128,128]{2,1,0:T(8,128)} fusion(f32[48,128,128]{2,1,0:T(8,128)S(1)} %pad_maximum_fusion, s32[1024]{0:T(1024)S(1)} %get-tuple-element.55), kind=kCustom, calls=%fused_computation.4 | custom fusion | bytes 2097216 | tf_op jit(solution)/shard_map/gather | solution.py:64
  37.1 1.6 %gather_fusion.5 = f32[16,128,128]{2,1,0:T(8,128)} fusion(f32[48,128,128]{2,1,0:T(8,128)S(1)} %pad_maximum_fusion, s32[1024]{0:T(1024)S(1)} %get-tuple-element.54), kind=kCustom, calls=%fused_computation.5 | custom fusion | bytes 2097216 | tf_op jit(solution)/shard_map/gather | solution.py:64
  38.7 1.6 %gather_fusion.6 = f32[16,128,128]{2,1,0:T(8,128)} fusion(f32[48,128,128]{2,1,0:T(8,128)S(1)} %pad_maximum_fusion, s32[1024]{0:T(1024)S(1)} %get-tuple-element.53), kind=kCustom, calls=%fused_computation.6 | custom fusion | bytes 2097216 | tf_op jit(solution)/shard_map/gather | solution.py:64
  40.3 1.6 %gather_fusion.7 = f32[16,128,128]{2,1,0:T(8,128)} fusion(f32[48,128,128]{2,1,0:T(8,128)S(1)} %pad_maximum_fusion, s32[1024]{0:T(1024)S(1)} %get-tuple-element.52), kind=kCustom, calls=%fused_computation.7 | custom fusion | bytes 2097216 | tf_op jit(solution)/shard_map/gather | solution.py:64
  41.9 7.7 %subtract_multiply_fusion = (f32[16,128,128]{2,1,0:T(8,128)}, f32[16,128,128]{2,1,0:T(8,128)}, f32[16,128,128]{2,1,0:T(8,128)}, f32[16,128,128]{2,1,0:T(8,128)},...) fusion(f32[16,128,128]{2,1,0:T(8,128)} %gather_fusion.7, ...), kind=kLoop, calls=%fused_computation.31 | loop fusion | flops 4194304 | bytes 17826304 | tf_op jit(solution)/shard_map/mul | solution.py:64
  49.6 0.4 broadcast_in_dim.15
  50.0 2.6 %scatter_fusion = f32[48,128,128]{2,1,0:T(8,128)S(1)} fusion(f32[48,128,128]{2,1,0:T(8,128)S(1)} %broadcast_in_dim.15, s32[16]{0:T(128)S(1)} %get-tuple-element.51, f32[16,128,128]{2,1,0:T(8,128)} %get-tuple-element.35), kind=kCustom, calls=%fused_computation.8 | custom fusion | flops 262144 | bytes 3145792 | tf_op jit(solution)/shard_map/scatter-add | solution.py:66
  52.6 2.6 %scatter_fusion.1 = f32[48,128,128]{2,1,0:T(8,128)S(1)} fusion(f32[48,128,128]{2,1,0:T(8,128)S(1)} %scatter_fusion, s32[16]{0:T(128)S(1)} %get-tuple-element.50, f32[16,128,128]{2,1,0:T(8,128)} %get-tuple-element.34), kind=kCustom, calls=%fused_computation.9 | custom fusion | flops 262144 | bytes 3145792 | tf_op jit(solution)/shard_map/scatter-add | solution.py:66
  55.2 2.6 %scatter_fusion.2 = f32[48,128,128]{2,1,0:T(8,128)S(1)} fusion(f32[48,128,128]{2,1,0:T(8,128)S(1)} %scatter_fusion.1, s32[16]{0:T(128)S(1)} %get-tuple-element.49, f32[16,128,128]{2,1,0:T(8,128)} %get-tuple-element.33), kind=kCustom, calls=%fused_computation.10 | custom fusion | flops 262144 | bytes 3145792 | tf_op jit(solution)/shard_map/scatter-add | solution.py:66
  57.8 2.6 %scatter_fusion.3 = f32[48,128,128]{2,1,0:T(8,128)S(1)} fusion(f32[48,128,128]{2,1,0:T(8,128)S(1)} %scatter_fusion.2, s32[16]{0:T(128)S(1)} %get-tuple-element.48, f32[16,128,128]{2,1,0:T(8,128)} %get-tuple-element.32), kind=kCustom, calls=%fused_computation.11 | custom fusion | flops 262144 | bytes 3145792 | tf_op jit(solution)/shard_map/scatter-add | solution.py:66
  60.5 2.6 %scatter_fusion.4 = f32[48,128,128]{2,1,0:T(8,128)S(1)} fusion(f32[48,128,128]{2,1,0:T(8,128)S(1)} %scatter_fusion.3, s32[16]{0:T(128)S(1)} %get-tuple-element.47, f32[16,128,128]{2,1,0:T(8,128)} %get-tuple-element.31), kind=kCustom, calls=%fused_computation.12 | custom fusion | flops 262144 | bytes 3145792 | tf_op jit(solution)/shard_map/scatter-add | solution.py:66
  63.1 2.6 %scatter_fusion.5 = f32[48,128,128]{2,1,0:T(8,128)S(1)} fusion(f32[48,128,128]{2,1,0:T(8,128)S(1)} %scatter_fusion.4, s32[16]{0:T(128)S(1)} %get-tuple-element.46, f32[16,128,128]{2,1,0:T(8,128)} %get-tuple-element.30), kind=kCustom, calls=%fused_computation.13 | custom fusion | flops 262144 | bytes 3145792 | tf_op jit(solution)/shard_map/scatter-add | solution.py:66
  65.7 2.6 %scatter_fusion.6 = f32[48,128,128]{2,1,0:T(8,128)S(1)} fusion(f32[48,128,128]{2,1,0:T(8,128)S(1)} %scatter_fusion.5, s32[16]{0:T(128)S(1)} %get-tuple-element.45, f32[16,128,128]{2,1,0:T(8,128)} %get-tuple-element.29), kind=kCustom, calls=%fused_computation.14 | custom fusion | flops 262144 | bytes 3145792 | tf_op jit(solution)/shard_map/scatter-add | solution.py:66
  68.3 2.6 %scatter_fusion.7 = f32[48,128,128]{2,1,0:T(8,128)S(1)} fusion(f32[48,128,128]{2,1,0:T(8,128)S(1)} %scatter_fusion.6, s32[16]{0:T(128)S(1)} %get-tuple-element.44, f32[16,128,128]{2,1,0:T(8,128)} %get-tuple-element.28), kind=kCustom, calls=%fused_computation.15 | custom fusion | flops 262144 | bytes 3145792 | tf_op jit(solution)/shard_map/scatter-add | solution.py:66
  71.3 2.9 %collective-permute-start.2 = (bf16[16,128,128]{2,1,0:T(8,128)(2,1)S(1)}, bf16[16,128,128]{2,1,0:T(8,128)(2,1)S(1)}, u32[]{:S(2)}, u32[]{:S(2)}) collective-permute-start(bf16[16,128,128]{2,1,0:T(8,128)(2,1)S(1)} %get-tuple-element.26), channel_id=1, source_target_pairs={{0,28},{4,0},{8,4},{12,8},{16,12},{20,16},{24,20},{28,24},{1,29},{... | collective-permute-start | bytes 1572872 | tf_op jit(solution)/shard_map/ppermute | solution.py:31
  74.3 12.2 %collective-permute-done.2 = bf16[16,128,128]{2,1,0:T(8,128)(2,1)S(1)} collective-permute-done((bf16[16,128,128]{2,1,0:T(8,128)(2,1)S(1)}, bf16[16,128,128]{2,1,0:T(8,128)(2,1)S(1)}, u32[]{:S(2)}, u32[]{:S(2)}) %collective-permute-start.2) | collective-permute-done | bytes 524320 | tf_op jit(solution)/shard_map/ppermute | solution.py:31
  86.5 0.4 collective-permute-done.3
  87.0 3.1 %fusion.6 = f32[16,128,128]{2,1,0:T(8,128)S(1)} fusion(f32[16,128,128]{2,1,0:T(8,128)} %bitcast.72, f32[48,128,128]{2,1,0:T(8,128)S(1)} %scatter_fusion.7, bf16[16,128,128]{2,1,0:T(8,128)(2,1)S(1)} %collective-permute-done.3, bf16[16,128,128]{2,1,0:T(8,128)(2,1)S(1)} %collective-permute-done.2, f32[16,128,128]{2,1,0:T(8,128)S(1)} %copy-done.1, ...), kind=kLoop, calls=%fused_computation.27 | loop fusion | flops 3407872 | bytes 12582912 | tf_op jit(solution)/shard_map/add | solution.py:70
  90.1 1.1 fusion.8
  91.1 4.7 %while.10 = (s32[]{:T(128)}, f32[2048,128]{1,0:T(8,128)S(1)}, bf16[128,128]{1,0:T(8,128)(2,1)S(1)}, s32[]{:T(128)}) while((s32[]{:T(128)}, f32[2048,128]{1,0:T(8,128)S(1)}, bf16[128,128]{1,0:T(8,128)(2,1)S(1)}, s32[]{:T(128)}) %tuple.53), condition=%wide.region_9.10_spmd, body=%wide.region_8.9_spmd.sunk | while | flops 67895296 | bytes 4227125 | solution.py:42
  91.2 0.3 fusion.38
  91.6 0.3 fusion.38
  92.0 0.3 fusion.38
  92.4 0.3 fusion.38
  93.2 0.3 fusion.38
  93.6 0.3 fusion.38
  94.3 0.3 fusion.38
  94.7 0.3 fusion.38
  95.5 0.3 fusion.38
  95.8 6.8 %scatter_custom_fusion.8 = bf16[4096,128]{1,0:T(8,128)(2,1)} fusion(s32[2048]{0:T(1024)S(1)} %bitcast.77, bf16[]{:T(256)} %constant.76.clone.1, f32[2048,128]{1,0:T(8,128)S(1)} %get-tuple-element.19), kind=kCustom, calls=%fused_computation.40 | custom fusion | flops 262144 | bytes 2097154 | tf_op jit(solution)/shard_map/scatter | solution.py:82
  102.6 5.6 %all-to-all-start = ((bf16[4,1024,128]{2,1,0:T(8,128)(2,1)}), bf16[4,1024,128]{2,1,0:T(8,128)(2,1)S(1)}, u32[]{:S(2)}, u32[]{:S(2)}) async-start(bf16[4,1024,128]{2,1,0:T(8,128)(2,1)} %bitcast.23), calls=%async_computation | async-start | bytes 2097152 | tf_op jit(solution)/shard_map/all_to_all | solution.py:84
  108.2 0.8 convert_element_type.36
  109.1 24.0 %all-to-all-done = bf16[4,1024,128]{2,1,0:T(8,128)(2,1)S(1)} async-done(((bf16[4,1024,128]{2,1,0:T(8,128)(2,1)}), bf16[4,1024,128]{2,1,0:T(8,128)(2,1)S(1)}, u32[]{:S(2)}, u32[]{:S(2)}) %all-to-all-start) | async-done | bytes 1048608 | tf_op jit(solution)/shard_map/all_to_all | solution.py:84
  133.0 1.0 copy.30
  (50 shorter events, 2.6 us)
Async XLA Ops:
  0.6 89.4 %copy-start = (f32[32,128]{1,0:T(8,128)S(1)}, f32[32,128]{1,0:T(8,128)}, u32[]{:S(2)}) copy-start(f32[32,128]{1,0:T(8,128)} %param.16) | copy-start | bytes 49156
  0.6 24.8 %collective-permute-start = (f32[16,128,128]{2,1,0:T(8,128)}, f32[16,128,128]{2,1,0:T(8,128)S(1)}, u32[]{:S(2)}, u32[]{:S(2)}) collective-permute-start(f32[16,128,128]{2,1,0:T(8,128)} %bitcast.68), channel_id=1, source_target_pairs={{0,4},{4,8},{8,12},{12,16},{16,20},{20,24},{24,28},{28,0},{1,5},{5... | collective-permute-start | bytes 3145736 | tf_op jit(solution)/shard_map/ppermute | solution.py:19
  1.2 25.8 %collective-permute-start.1 = (f32[16,128,128]{2,1,0:T(8,128)}, f32[16,128,128]{2,1,0:T(8,128)}, u32[]{:S(2)}, u32[]{:S(2)}) collective-permute-start(f32[16,128,128]{2,1,0:T(8,128)} %bitcast.69), channel_id=1, source_target_pairs={{4,0},{8,4},{12,8},{16,12},{20,16},{24,20},{28,24},{0,28},{5,1},{9... | collective-permute-start | bytes 3145736 | tf_op jit(solution)/shard_map/ppermute | solution.py:21
  25.4 1.0 copy-start.7
  70.9 3.3 %copy-start.9 = (s32[2048,1]{0,1:T(1,128)S(1)}, s32[2048,1]{0,1:T(1,128)}, u32[]{:S(2)}) copy-start(s32[2048,1]{0,1:T(1,128)} %param.15) | copy-start | bytes 24580
  70.9 16.0 %copy-start.1 = (f32[16,128,128]{2,1,0:T(8,128)S(1)}, f32[16,128,128]{2,1,0:T(8,128)}, u32[]{:S(2)}) copy-start(f32[16,128,128]{2,1,0:T(8,128)} %get-tuple-element.28) | copy-start | bytes 3145732
  70.9 16.0 %copy-start.2 = (f32[16,128,128]{2,1,0:T(8,128)S(1)}, f32[16,128,128]{2,1,0:T(8,128)}, u32[]{:S(2)}) copy-start(f32[16,128,128]{2,1,0:T(8,128)} %get-tuple-element.29) | copy-start | bytes 3145732
  71.0 16.0 %copy-start.3 = (f32[16,128,128]{2,1,0:T(8,128)S(1)}, f32[16,128,128]{2,1,0:T(8,128)}, u32[]{:S(2)}) copy-start(f32[16,128,128]{2,1,0:T(8,128)} %get-tuple-element.30) | copy-start | bytes 3145732
  71.0 16.0 %copy-start.4 = (f32[16,128,128]{2,1,0:T(8,128)S(1)}, f32[16,128,128]{2,1,0:T(8,128)}, u32[]{:S(2)}) copy-start(f32[16,128,128]{2,1,0:T(8,128)} %get-tuple-element.31) | copy-start | bytes 3145732
  71.0 16.0 %copy-start.5 = (f32[16,128,128]{2,1,0:T(8,128)S(1)}, f32[16,128,128]{2,1,0:T(8,128)}, u32[]{:S(2)}) copy-start(f32[16,128,128]{2,1,0:T(8,128)} %get-tuple-element.32) | copy-start | bytes 3145732
  71.0 16.0 %copy-start.6 = (f32[16,128,128]{2,1,0:T(8,128)S(1)}, f32[16,128,128]{2,1,0:T(8,128)}, u32[]{:S(2)}) copy-start(f32[16,128,128]{2,1,0:T(8,128)} %get-tuple-element.33) | copy-start | bytes 3145732
  71.3 15.2 %collective-permute-start.2 = (bf16[16,128,128]{2,1,0:T(8,128)(2,1)S(1)}, bf16[16,128,128]{2,1,0:T(8,128)(2,1)S(1)}, u32[]{:S(2)}, u32[]{:S(2)}) collective-permute-start(bf16[16,128,128]{2,1,0:T(8,128)(2,1)S(1)} %get-tuple-element.26), channel_id=1, source_target_pairs={{0,28},{4,0},{8,4},{12,8},{16,12},{20,16},{24,20},{28,24},{1,29},{... | collective-permute-start | bytes 1572872 | tf_op jit(solution)/shard_map/ppermute | solution.py:31
  74.2 12.7 %collective-permute-start.3 = (bf16[16,128,128]{2,1,0:T(8,128)(2,1)S(1)}, bf16[16,128,128]{2,1,0:T(8,128)(2,1)S(1)}, u32[]{:S(2)}, u32[]{:S(2)}) collective-permute-start(bf16[16,128,128]{2,1,0:T(8,128)(2,1)S(1)} %get-tuple-element.27), channel_id=1, source_target_pairs={{0,4},{4,8},{8,12},{12,16},{16,20},{20,24},{24,28},{28,0},{1,5},{5... | collective-permute-start | bytes 1572872 | tf_op jit(solution)/shard_map/ppermute | solution.py:31
  74.3 15.8 %copy-start.10 = (s32[2048]{0:T(1024)S(1)}, s32[2048]{0:T(1024)}, u32[]{:S(2)}) copy-start(s32[2048]{0:T(1024)} %param.14) | copy-start | bytes 24580
  74.3 16.9 %copy-start.8 = (bf16[128,128]{1,0:T(8,128)(2,1)S(1)}, bf16[128,128]{1,0:T(8,128)(2,1)}, u32[]{:S(2)}) copy-start(bf16[128,128]{1,0:T(8,128)(2,1)} %param.17) | copy-start | bytes 98308
  102.6 30.5 %all-to-all-start = ((bf16[4,1024,128]{2,1,0:T(8,128)(2,1)}), bf16[4,1024,128]{2,1,0:T(8,128)(2,1)S(1)}, u32[]{:S(2)}, u32[]{:S(2)}) async-start(bf16[4,1024,128]{2,1,0:T(8,128)(2,1)} %bitcast.23), calls=%async_computation | async-start | bytes 2097152 | tf_op jit(solution)/shard_map/all_to_all | solution.py:84
where the time goes:
time: 135 us; the launch traced here: 134 us
  waiting for transfers between devices  54.7 us (41%)
  other arithmetic  45.2 us (33%)
  local copies, waits for them, and re-layouts  16.3 us (12%)
  starting transfers between devices  12 us (9%)
  matrix products  4.51 us (3%)
    all_to_all x1, waiting for transfers between devices, shards(): lax.all_to_all(outgoing, 'bal', split_axis=0, concat_axis=0, tiled=True)  24 us
    scatter-add x8, other arithmetic, shards(): sent = sent.at[ext_index[:, column]].add(flux)  20.9 us
    ppermute x1, waiting for transfers between devices, extended_2(): lax.ppermute(tail, axis, [(i, (i + 1) % count) for i in range(count)])  17.5 us
    gather x8, local copies, waits for them, and re-layouts, shards(): extended[ext_index[:, column]] - own_blocks  12.9 us
    ppermute x2, waiting for transfers between devices, shifted(): return lax.ppermute(value, axis, pairs)  12.6 us
    mul x1, other arithmetic, shards(): coefs[:, column][:, None, None]  7.75 us
    scatter x1, other arithmetic, shards(): jnp.zeros((bal_count * capacity, width), jnp.bfloat16).at[slot]  6.78 us
    all_to_all x1, starting transfers between devices, shards(): lax.all_to_all(outgoing, 'bal', split_axis=0, concat_axis=0, tiled=True)  5.63 us
  transfers between devices with their start and end apart: 5, of which 5 were waited for; matrix products, arithmetic and copies ran while one was open for 3% of the time, Pallas kernels for 0%

commit v1 on v0

v1 whole, which is shorter than its diff:
```python
import functools

import jax
import jax.numpy as jnp
from jax import lax
from jax.experimental import pallas as pl
from jax.experimental.pallas import tpu as pltpu
from jax.sharding import PartitionSpec as P


BLK = 128
LANES = 128
TILE = 16
SHIFT = 4
ZONES = 32
SUBSTEPS = 12
CHUNKS = 2
LOADS = 4
TILES = 4

F32 = jnp.float32
BF16 = jnp.bfloat16
VMEM = pl.BlockSpec(memory_space=pltpu.VMEM)
SMEM = pl.BlockSpec(memory_space=pltpu.SMEM)
ANY = pl.BlockSpec(memory_space=pl.ANY)
HBM = pl.BlockSpec(memory_space=pltpu.HBM)


def iota(shape, axis):
    return lax.broadcasted_iota(jnp.int32, shape, axis)


def dot(a, b):
    return jnp.dot(a, b, preferred_element_type=F32)


def dot_first(a, b):
    return lax.dot_general(a, b, (((0,), (0,)), ((), ())), preferred_element_type=F32)


def eye(rows, shift=0):
    shape = (rows, LANES)
    return jnp.where(iota(shape, 0) + shift == iota(shape, 1), 1.0, 0.0).astype(BF16)


def regroup(parts, source, chunks):
    width = LANES // chunks
    group = lax.shift_right_logical(iota(parts[0].shape, 1), width.bit_length() - 1)
    out = None
    for place in range(chunks):
        moved = parts[place]
        turn = (place - source) % chunks * width
        if turn:
            moved = pltpu.roll(moved, turn, 1)
        out = moved if out is None else jnp.where(group == place, moved, out)
    return out


def load_all(source, target, sems):
    rows = target.shape[0] // LOADS
    copies = [
        pltpu.make_async_copy(
            source.at[pl.ds(i * rows, rows)], target.at[pl.ds(i * rows, rows)], sems.at[i]
        )
        for i in range(LOADS)
    ]
    for copy in copies:
        copy.start()
    return copies


def pack_kernel(chunks, chunk, nblocks, conc, *refs):
    span = BLK // chunks
    if chunk == 0:
        lists, msg, table, held = refs[:3], refs[3], refs[4], refs[5:8]
        stage, buffer, sems = refs[8:]
        small = [
            pltpu.make_async_copy(source, target, sems.at[2 * LOADS + 1 + i])
            for i, (source, target) in enumerate(zip(lists, held))
        ]
        for copy in small:
            copy.start()
        neighbours, counts, weights = held
    else:
        msg, stage, buffer, sems = refs
    loads = load_all(conc, stage, sems)
    stores = []

    def store(i, first, rows):
        copy = pltpu.make_async_copy(
            buffer.at[pl.ds(first, rows)], msg.at[pl.ds(first, rows)], sems.at[LOADS + i]
        )
        copy.start()
        stores.append(copy)

    if chunk == 0:
        for copy in small:
            copy.wait()
        nlon, nbal = lax.axis_size("lon"), lax.axis_size("bal")
        me = lax.axis_index("lon") * nbal + lax.axis_index("bal")
        column = iota((3 * nblocks, nblocks), 0)
        pairs = jnp.zeros((3 * nblocks, nblocks), jnp.int32)
        for k in range(neighbours.shape[0]):
            target = neighbours[k : k + 1, :]
            device = lax.div(target, nblocks)
            apart = device - me
            right = (apart == nbal) | (apart == nbal - nlon * nbal)
            place = jnp.where(apart == 0, 0, jnp.where(right, 2 * nblocks, nblocks))
            place = place + target - device * nblocks
            weight = jnp.where(k < counts[...], weights[k : k + 1, :], 0)
            pairs = pairs + jnp.where(column == place, weight, 0)
        pairs = jnp.where(column == iota(column.shape, 1), 0, pairs)
        pairs = (pairs.astype(F32) * (1.0 / BLK)).astype(BF16)
        table[...] = dot_first(pairs, eye(3 * nblocks)) + dot(pairs[:nblocks], eye(nblocks))
        carried = dot(pairs[2 * nblocks :], eye(nblocks, nblocks))
        carried = carried + dot(pairs[nblocks : 2 * nblocks], eye(nblocks, 2 * nblocks))
        buffer[nblocks * span :, :] = carried.astype(BF16)
        store(LOADS, nblocks * span, nblocks)
    each = nblocks // LOADS
    for i in range(LOADS):
        loads[i].wait()
        for b in range(i * each, (i + 1) * each):
            rows = [stage[b * BLK + j * span : b * BLK + (j + 1) * span, :] for j in range(chunks)]
            buffer[b * span : (b + 1) * span, :] = regroup(rows, chunk, chunks).astype(BF16)
        store(i, i * each * span, each * span)
    for copy in stores:
        copy.wait()


def tall(value, rows):
    nblocks = value.shape[0]
    value = jnp.broadcast_to(value, (nblocks, LANES))
    wide = jnp.broadcast_to(value[:, None, :], (nblocks, rows, LANES))
    return wide.reshape(nblocks * rows, LANES)


def couple(table, first, blocks, nblocks):
    columns = blocks * TILE
    pick = (iota((LANES, columns), 1) >> SHIFT) + first == iota((LANES, columns), 0)
    wide = dot(table.astype(BF16), jnp.where(pick, 1.0, 0.0).astype(BF16))
    same = iota((TILE, LANES), 0) == (iota((TILE, LANES), 1) & (TILE - 1))
    same = jnp.where(same, 1.0, 0.0)
    parts = []
    for c in range(0, columns, LANES):
        part = jnp.broadcast_to(wide[:, None, c : c + LANES], (nblocks, TILE, LANES)) * same[None]
        parts.append(part.reshape(nblocks * TILE, LANES).astype(BF16))
    return jnp.concatenate(parts, axis=1)


def pieces(ref, u, nblocks, span):
    tiles = [
        jnp.concatenate(
            [ref[b * span + v * TILE : b * span + (v + 1) * TILE, :] for b in range(nblocks)], axis=0
        )
        for v in (u, u + 1)
    ]
    return jnp.concatenate(tiles, axis=1)


def prepare_kernel(chunks, chunk, nblocks, nbal, zones, rates, table, conc, *refs):
    span, width = BLK // chunks, LANES // chunks
    if chunk == 0:
        owners, factor, kept, keys, bases, stage, value, sems = refs
    else:
        factor, kept, stage, value, sems = refs
    loads = load_all(conc, stage, sems)

    decay = jnp.exp(-rates[...])
    lane = iota((span, LANES), 1)
    group = lax.shift_right_logical(lane, ZONES.bit_length() - 1)
    rows = []
    for j in range(chunks):
        turn = (j - chunk) % chunks * width
        moved = pltpu.roll(decay, turn, 1) if turn else decay
        rows.append(jnp.where(lax.shift_right_logical(iota(moved.shape, 1), width.bit_length() - 1) == j, moved, 0.0))
    if chunks * ZONES < LANES:
        rows.append(jnp.zeros((LANES - chunks * ZONES, LANES), F32))
    spread = jnp.concatenate(rows, axis=0)
    high = spread.astype(BF16)
    low = (spread - high.astype(F32)).astype(BF16)
    both = jnp.concatenate([high, low], axis=0)
    upright = dot_first(zones[...].astype(F32).astype(BF16), eye(nblocks))
    for b in range(nblocks):
        column = jnp.broadcast_to(upright[:, b : b + 1], (BLK, LANES))
        picked = column[:span]
        for j in range(1, chunks):
            picked = jnp.where(group == j, column[j * span : (j + 1) * span], picked)
        own = (picked == (lane - group * ZONES).astype(F32)) & (group < chunks)
        own = jnp.where(own, 1.0, 0.0).astype(BF16)
        factor[b] = dot(jnp.concatenate([own, own], axis=1), both)

    if chunk == 0:
        before = jnp.where(iota((BLK, LANES), 0) < iota((BLK, LANES), 1), 1.0, 0.0).astype(BF16)
        above = jnp.where(iota((nblocks, nblocks), 1) < iota((nblocks, nblocks), 0), 1.0, 0.0)
        windows = jnp.zeros((nblocks, LANES), F32)
        slot_lane = iota((nblocks, LANES), 1)
        relative = jnp.bitwise_xor(owners[...], lax.axis_index("bal"))
        step = TILE * chunks
        for k in range(nbal):
            mine = relative == k
            narrow = jnp.where(mine, 1.0, 0.0).astype(BF16)
            rank = dot(narrow, before)
            start = jnp.sum(dot(above.astype(BF16), narrow), axis=1, keepdims=True)
            window = jnp.floor(start * (1.0 / step))
            keys[k] = jnp.where(mine, rank + (start - window * step), -1.0)
            windows = jnp.where(slot_lane == k, window * TILE, windows)
        bases[...] = windows.astype(jnp.int32)

    coupling = table[...]
    kron = couple(coupling, 0, nblocks, nblocks)
    lane = iota((nblocks, LANES), 1)
    inner = jnp.sum(jnp.where(lane < nblocks, coupling, 0.0), axis=1, keepdims=True)
    keep = tall(1.0 - inner, TILE)
    each = nblocks // LOADS
    for i in range(LOADS):
        loads[i].wait()
        for b in range(i * each, (i + 1) * each):
            rows = [stage[b * BLK + j * span : b * BLK + (j + 1) * span, :] for j in range(chunks)]
            value[b * span : (b + 1) * span, :] = regroup(rows, chunk, chunks)
    for u in range(0, span // TILE, 2):
        whole = pieces(value, u, nblocks, span)
        high = whole.astype(BF16)
        low = (whole - high.astype(F32)).astype(BF16)
        total = dot(kron, high) + dot(kron, low)
        for v in range(2):
            side = slice(v * LANES, (v + 1) * LANES)
            part = total[:, side] + keep * whole[:, side]
            for b in range(nblocks):
                kept[b, (u + v) * TILE : (u + v + 1) * TILE, :] = part[b * TILE : (b + 1) * TILE]


def mix_kernel(chunks, chunk, nblocks, nbal, bases, left, right, table, high, kept, factor, keys, *refs):
    span, width = BLK // chunks, LANES // chunks
    rows = nblocks * span
    start, slots = refs[0], refs[1:nbal]
    buffer = refs[-1]
    lane = iota((nblocks, LANES), 1)
    coupling = table[...]
    if chunk == 0:
        from_left = left[rows : rows + nblocks, :].astype(F32)
        from_right = right[rows : rows + nblocks, :].astype(F32)
        coupling = coupling + jnp.where((lane >= nblocks) & (lane < 2 * nblocks), from_left, 0.0)
        coupling = coupling + jnp.where((lane >= 2 * nblocks) & (lane < 3 * nblocks), from_right, 0.0)
        refs[nbal][...] = coupling
    outer = jnp.sum(jnp.where(lane < nblocks, 0.0, coupling), axis=1, keepdims=True)
    outer = tall(outer, TILE)
    kron = couple(coupling, nblocks, 2 * nblocks, nblocks)
    edge = nblocks * TILE

    for u in range(0, span // TILE, 2):
        total = dot(kron[:, :edge], pieces(left, u, nblocks, span))
        total = total + dot(kron[:, edge:], pieces(right, u, nblocks, span))
        for v in range(2):
            at = slice((u + v) * TILE, (u + v + 1) * TILE)
            for b in range(nblocks):
                mine = high[b * span + (u + v) * TILE : b * span + (u + v + 1) * TILE, :].astype(F32)
                tile = slice(b * TILE, (b + 1) * TILE)
                mixed = total[tile, v * LANES : (v + 1) * LANES] + kept[b, at, :]
                mixed = mixed - outer[tile] * mine
                start[b, at, :] = (mixed * factor[b, at, :]).astype(BF16)

    reach = span + TILE
    depth = slots[0].shape[0]
    buffer[...] = jnp.zeros(buffer.shape, BF16)
    line = iota((reach, LANES), 0)
    marks = [
        ((line >> SHIFT) * (TILE * chunks) + jj * TILE + (line & (TILE - 1))).astype(F32)
        for jj in range(chunks)
    ]
    group = lax.shift_right_logical(iota((reach, LANES), 1), width.bit_length() - 1)
    for b in range(nblocks):
        select = []
        for k in range(1, nbal):
            key = jnp.broadcast_to(keys[k, b : b + 1, :], (reach, LANES))
            select += [jnp.where(key == m, 1.0, 0.0).astype(BF16) for m in marks]
        block = start[b].astype(F32)
        spread = [regroup([block] * chunks, j, chunks).astype(BF16) for j in range(chunks)]
        placed = dot(jnp.concatenate(select, axis=0), jnp.concatenate(spread, axis=0))
        for k in range(1, nbal):
            first = (k - 1) * chunks * reach
            window = placed[first : first + reach]
            for jj in range(1, chunks):
                other = placed[first + jj * reach : first + (jj + 1) * reach]
                window = jnp.where(group == jj, other, window)
            window = window.astype(BF16)
            at = pl.multiple_of(bases[b, k], TILE)
            buffer[k - 1, pl.ds(at, TILE), :] = buffer[k - 1, pl.ds(at, TILE), :] + window[:TILE]
            buffer[k - 1, pl.ds(at + TILE, span), :] = window[TILE:]
    for k in range(1, nbal):
        slots[k - 1][...] = buffer[k - 1, :depth, :]


def chemistry(state, reaction):
    quarter = (reaction[...].astype(F32) * 0.25).astype(BF16)
    rows = state.shape[0] // TILES
    for _ in range(SUBSTEPS):
        for t in range(TILES):
            current = state[t * rows : (t + 1) * rows, :]
            tendency = dot(current.astype(BF16), quarter)
            state[t * rows : (t + 1) * rows, :] = current + jnp.tanh(tendency)


def own_kernel(chunks, nblocks, bases, reaction, keys, *refs):
    starts, out, slots, state, done, buffer, sem = refs[:chunks], *refs[chunks:]
    span = BLK // chunks
    for b in range(nblocks):
        rows = [starts[c][b].astype(F32) * 4.0 for c in range(chunks)]
        for j in range(chunks):
            first = b * BLK + j * span
            state[first : first + span, :] = regroup(rows, j, chunks)
    chemistry(state, reaction)
    done[...] = (state[...] * 0.25).astype(BF16)
    out[...] = done[...]
    reach = BLK + TILE * chunks
    capacity = slots.shape[1] * slots.shape[2] * slots.shape[3]
    buffer[...] = jnp.zeros(buffer.shape, BF16)
    mark = iota((reach, LANES), 0).astype(F32)
    for b in range(nblocks):
        key = jnp.broadcast_to(keys[0, b : b + 1, :], (reach, LANES))
        select = jnp.where(key == mark, 1.0, 0.0).astype(BF16)
        window = dot(select, done[b * BLK : (b + 1) * BLK, :]).astype(BF16)
        at = pl.multiple_of(bases[b, 0] * chunks, TILE)
        edge = TILE * chunks
        buffer[pl.ds(at, edge), :] = buffer[pl.ds(at, edge), :] + window[:edge]
        buffer[pl.ds(at + edge, BLK), :] = window[edge:]
    for _ in range(1):
        copy = pltpu.make_async_copy(
            buffer.at[pl.ds(0, capacity)].reshape(slots.shape[1:]), slots.at[lax.axis_index("bal")], sem
        )
        copy.start()
        copy.wait()


def slot_kernel(chunks, k, reaction, *refs):
    parts = refs[:chunks]
    out, state, result, sem = refs[-4:]
    depth = parts[0].shape[0]
    rows = [part[...].astype(F32) * 4.0 for part in parts]
    for jj in range(chunks):
        state[jj * depth : (jj + 1) * depth, :] = regroup(rows, jj, chunks)
    chemistry(state, reaction)
    for jj in range(chunks):
        done = (state[jj * depth : (jj + 1) * depth, :] * 0.25).astype(BF16)
        result[:, jj] = done.reshape(depth // TILE, TILE, LANES)
    place = jnp.bitwise_xor(lax.axis_index("bal"), k)
    copy = pltpu.make_async_copy(result, out.at[place], sem)
    copy.start()
    copy.wait()


def ORDER(nbal):
    return [k for k in range(1, nbal) if k != 2] + [2]


def step(conc, neighbours, counts, weights, zones, owners, rate_table, reaction):
    rows, width = conc.shape
    nblocks = rows // BLK
    nlon, nbal = lax.axis_size("lon"), lax.axis_size("bal")
    chunks = CHUNKS
    span = BLK // chunks
    capacity = 2 * rows // nbal
    depth = capacity // chunks

    shape = jax.ShapeDtypeStruct
    zones, owners = zones.reshape(nblocks, BLK), owners.reshape(nblocks, BLK)
    blocked = shape((nblocks, span, LANES), F32)

    def call(body, limit=16, **kw):
        params = pltpu.CompilerParams(vmem_limit_bytes=limit << 20)
        return pl.pallas_call(body, compiler_params=params, **kw)

    ahead = [(i, (i + 1) % nlon) for i in range(nlon)]
    back = [((i + 1) % nlon, i) for i in range(nlon)]
    lists = (neighbours.T, counts.reshape(1, nblocks), weights.T)
    msgs, lefts, rights, table = [], [], [], None
    for c in range(chunks):
        first = c == 0
        length = nblocks * span + (nblocks if first else 0)
        outs = call(
            functools.partial(pack_kernel, chunks, c, nblocks),
            60 if first else 16,
            out_shape=[shape((length, LANES), BF16)] + [shape((nblocks, LANES), F32)] * first,
            in_specs=[HBM] * (1 + 3 * first),
            out_specs=[ANY] + [VMEM] * first,
            scratch_shapes=[pltpu.VMEM(a.shape, jnp.int32) for a in lists if first]
            + [
                pltpu.VMEM((rows, LANES), F32),
                pltpu.VMEM((length, LANES), BF16),
                pltpu.SemaphoreType.DMA((2 * LOADS + 4,)),
            ],
        )(conc, *(lists if first else ()))
        if first:
            table = outs[1]
        msgs.append(outs[0])
        lefts.append(lax.ppermute(outs[0], "lon", ahead))
        rights.append(lax.ppermute(outs[0], "lon", back))

    factors, kepts, keys, bases = [], [], None, None
    for c in range(chunks):
        first = c == 0
        outs = call(
            functools.partial(prepare_kernel, chunks, c, nblocks, nbal),
            out_shape=[blocked, blocked]
            + [shape((nbal, nblocks, LANES), F32), shape((nblocks, LANES), jnp.int32)] * first,
            in_specs=[VMEM] * 3 + [HBM] + [VMEM] * first,
            out_specs=[VMEM] * (2 + 2 * first),
            scratch_shapes=[
                pltpu.VMEM((rows, LANES), F32),
                pltpu.VMEM((nblocks * span, LANES), F32),
                pltpu.SemaphoreType.DMA((LOADS,)),
            ],
        )(zones, rate_table, table, conc, *([owners] if first else []))
        factors.append(outs[0])
        kepts.append(outs[1])
        if first:
            keys, bases = outs[2:]

    starts, received = [], [[None] * chunks for _ in range(nbal)]
    for c in range(chunks):
        first = c == 0
        outs = call(
            functools.partial(mix_kernel, chunks, c, nblocks, nbal),
            out_shape=[shape((nblocks, span, LANES), BF16)]
            + [shape((depth, LANES), BF16)] * (nbal - 1)
            + [shape((nblocks, LANES), F32)] * first,
            in_specs=[SMEM] + [VMEM] * 7,
            out_specs=[VMEM] * (nbal + first),
            scratch_shapes=[pltpu.VMEM((nbal - 1, depth + span + TILE, LANES), BF16)],
        )(bases, lefts[c], rights[c], table, msgs[c], kepts[c], factors[c], keys)
        starts.append(outs[0])
        if first:
            table = outs[nbal]
        for k in range(1, nbal):
            received[k][c] = lax.ppermute(outs[k], "bal", [(i, i ^ k) for i in range(nbal)])

    tiles = shape((nbal, depth // TILE, chunks, TILE, LANES), BF16)
    conc_out, chem = call(
        functools.partial(own_kernel, chunks, nblocks),
        out_shape=[shape((rows, LANES), BF16), tiles],
        in_specs=[SMEM] + [VMEM] * (2 + chunks),
        out_specs=[VMEM, ANY],
        scratch_shapes=[
            pltpu.VMEM((rows, LANES), F32),
            pltpu.VMEM((rows, LANES), BF16),
            pltpu.VMEM((capacity + BLK + TILE * chunks, LANES), BF16),
            pltpu.SemaphoreType.DMA,
        ],
    )(bases, reaction, keys, *starts)
    for k in ORDER(nbal):
        chem = call(
            functools.partial(slot_kernel, chunks, k),
            out_shape=tiles,
            in_specs=[VMEM] * (1 + chunks) + [ANY],
            out_specs=ANY,
            scratch_shapes=[
                pltpu.VMEM((capacity, LANES), F32),
                pltpu.VMEM(tiles.shape[1:], BF16),
                pltpu.SemaphoreType.DMA,
            ],
            input_output_aliases={1 + chunks: 0},
        )(reaction, *received[k], chem)
    return conc_out, chem.reshape(nbal * capacity, width)


def solution(mesh):
    in_specs = (
        P(("lon", "bal"), None),
        P(("lon", "bal"), None),
        P(("lon", "bal")),
        P(("lon", "bal"), None),
        P(("lon", "bal")),
        P(("lon", "bal"), None),
        P(),
        P(),
    )
    out_specs = (P(("lon", "bal"), None), P(("lon", "bal"), None))
    return jax.shard_map(step, mesh=mesh, in_specs=in_specs, out_specs=out_specs, check_vma=False)
```

time: 135 us -> 49.2 us (0.36)
  other arithmetic: 45.2 us -> 0 us
  waiting for transfers between devices: 54.7 us -> 10.5 us
  Pallas kernels: 0 us -> 22.3 us
  local copies, waits for them, and re-layouts: 16.3 us -> 0.03 us
  matrix products: 4.51 us -> 0 us
  starting transfers between devices: 12 us -> 15.5 us
    all_to_all x1 -> x0, waiting for transfers between devices: 24 us -> none  [shards(): lax.all_to_all(outgoing, 'bal', split_axis=0, concat_axis=0, tiled=True)]
    pallas_call x0 -> x10, Pallas kernels: none -> 22.3 us  [the longest x3 7.23 us: step(): call(functools.partial(slot_kernel, chunks, k), out_shape=tiles, in_specs...]
    scatter-add x8 -> x0, other arithmetic: 20.9 us -> none  [shards(): sent = sent.at[ext_index[:, column]].add(flux)]
    ppermute x4 -> x10, waiting for transfers between devices: 30.7 us -> 10.5 us  [the longest x6 8.63 us: step(): lax.ppermute(outs[k], 'bal', [(i, i ^ k) for i in range(nbal)])]
    gather x8 -> x0, local copies, waits for them, and re-layouts: 12.9 us -> none  [shards(): extended[ext_index[:, column]] - own_blocks]
    ppermute x4 -> x10, starting transfers between devices: 6.34 us -> 15.5 us  [the longest x6 9.33 us: step(): lax.ppermute(outs[k], 'bal', [(i, i ^ k) for i in range(nbal)])]
    mul x1 -> x0, other arithmetic: 7.75 us -> none  [shards(): coefs[:, column][:, None, None]]
    scatter x1 -> x0, other arithmetic: 6.78 us -> none  [shards(): jnp.zeros((bal_count * capacity, width), jnp.bfloat16).at[slot]]
  transfers between devices with their start and end apart: 5 -> 10, of which waited for: 5 -> 3; matrix products, arithmetic and copies ran while one was open for 3% -> 0% of each run, Pallas kernels for 0% -> 35%
where the time goes in v1:
time: 49.2 us; the launch traced here: 49.1 us
  Pallas kernels  22.3 us (45%)
  starting transfers between devices  15.5 us (32%)
  waiting for transfers between devices  10.5 us (21%)
  between operations  0.79 us (2%)
    ppermute x6, starting transfers between devices, step(): lax.ppermute(outs[k], 'bal', [(i, i ^ k) for i in range(nbal)])  9.33 us
    ppermute x6, waiting for transfers between devices, step(): lax.ppermute(outs[k], 'bal', [(i, i ^ k) for i in range(nbal)])  8.63 us
    pallas_call x3, Pallas kernels, step(): call(functools.partial(slot_kernel, chunks, k), out_shape=tiles, in_specs...  7.23 us
    ppermute x2, starting transfers between devices, step(): rights.append(lax.ppermute(outs[0], 'lon', back))  5.57 us
    pallas_call x1, Pallas kernels, step(): call(functools.partial(own_kernel, chunks, nblocks), out_shape=[shape((ro...  4.44 us
    pallas_call x2, Pallas kernels, step(): call(functools.partial(mix_kernel, chunks, c, nblocks, nbal), out_shape=[...  3.78 us
    pallas_call x2, Pallas kernels, step(): call(functools.partial(pack_kernel, chunks, c, nblocks), 60 if first else...  3.64 us
    pallas_call x2, Pallas kernels, step(): call(functools.partial(prepare_kernel, chunks, c, nblocks, nbal), out_sha...  3.18 us
  transfers between devices with their start and end apart: 10, of which 3 were waited for; matrix products, arithmetic and copies ran while one was open for 0% of the time, Pallas kernels for 35%

profile of v1, /device:TPU:0, one launch (start us, length us, event | category | flops | bytes accessed | tf_op | source)
XLA Modules:
  0.0 49.1 jit_solution(15636956641635353119)
XLA Ops:
  0.6 0.0 copy-start
  0.6 2.8 %shard_map.95 = (bf16[1040,128]{1,0:T(8,128)(2,1)}, f32[16,128]{1,0:T(8,128)}) custom-call(f32[2048,128]{1,0:T(8,128)} %conc.7, s32[8,16]{1,0:T(8,128)} %bitcast.10, s32[1,16]{1,0:T(1,128)} %bitcast.12, s32[8,16]{1,0:T(8,128)} %bitcast.11), custom_call_target="tpu_custom_call" | custom-call | tf_op jit(solution)/shard_map/pallas_call | solution.py:379
  3.4 0.5 %collective-permute-start = (bf16[1040,128]{1,0:T(8,128)(2,1)}, bf16[1040,128]{1,0:T(8,128)(2,1)S(1)}, u32[]{:S(2)}, u32[]{:S(2)}) collective-permute-start(bf16[1040,128]{1,0:T(8,128)(2,1)} %get-tuple-element.24.high), channel_id=1, source_target_pairs={{0,4},{4,8},{8,12},{12,16},{16,20},{20,24},{24,28},{28,0},{1,5},{5... | collective-permute-start | bytes 798728 | tf_op jit(solution)/shard_map/ppermute | solution.py:395
  4.0 2.9 %collective-permute-start.1 = (bf16[1040,128]{1,0:T(8,128)(2,1)}, bf16[1040,128]{1,0:T(8,128)(2,1)S(1)}, u32[]{:S(2)}, u32[]{:S(2)}) collective-permute-start(bf16[1040,128]{1,0:T(8,128)(2,1)} %get-tuple-element.24.high), channel_id=1, source_target_pairs={{4,0},{8,4},{12,8},{16,12},{20,16},{24,20},{28,24},{0,28},{5,1},{9... | collective-permute-start | bytes 798728 | tf_op jit(solution)/shard_map/ppermute | solution.py:396
  6.9 0.0 copy-done
  6.9 0.0 copy-start.3
  6.9 0.0 copy-start.4
  6.9 0.0 copy-start.5
  6.9 0.0 copy-start.6
  6.9 0.9 %shard_map.98.high = bf16[1024,128]{1,0:T(8,128)(2,1)S(1)} custom-call(f32[2048,128]{1,0:T(8,128)S(1)} %copy-done), custom_call_target="tpu_custom_call" | custom-call | tf_op jit(solution)/shard_map/pallas_call | solution.py:379
  7.8 0.1 collective-permute-start.2
  7.9 2.6 %collective-permute-start.3 = (bf16[1024,128]{1,0:T(8,128)(2,1)S(1)}, bf16[1024,128]{1,0:T(8,128)(2,1)S(1)}, u32[]{:S(2)}, u32[]{:S(2)}) collective-permute-start(bf16[1024,128]{1,0:T(8,128)(2,1)S(1)} %shard_map.98.high), channel_id=1, source_target_pairs={{4,0},{8,4},{12,8},{16,12},{20,16},{24,20},{28,24},{0,28},{5,1},{9... | collective-permute-start | bytes 786440 | tf_op jit(solution)/shard_map/ppermute | solution.py:396
  10.5 0.0 copy-done.3
  10.5 0.0 copy-done.4
  10.5 0.0 copy-done.5
  10.5 0.0 copy-done.6
  10.5 0.0 copy-start.2
  10.5 1.6 %shard_map.96 = (f32[16,64,128]{2,1,0:T(8,128)S(1)}, f32[16,64,128]{2,1,0:T(8,128)S(1)}, f32[4,16,128]{2,1,0:T(8,128)S(1)}, s32[16,128]{1,0:T(8,128)S(1)}) custom-call(s32[16,128]{1,0:T(8,128)S(1)} %bitcast.6, f32[32,128]{1,0:T(8,128)S(1)} %copy-done.4, f32[16,128]{1,0:T(8,128)S(1)} %copy-done.3, f32[2048,128]{1,0:T(8,128)S(1)} %copy-done, s32[16,128]{1,0:T(8,128)S(1)} %bitcast.8), custom_call_target="tpu_custom_call" | custom-call | tf_op jit(solution)/shard_map/pallas_call | solution.py:401
  12.2 0.0 collective-permute-done.left
  12.2 1.8 %collective-permute-done.1.right = bf16[1040,128]{1,0:T(8,128)(2,1)S(1)} collective-permute-done((bf16[1040,128]{1,0:T(8,128)(2,1)}, bf16[1040,128]{1,0:T(8,128)(2,1)S(1)}, u32[]{:S(2)}, u32[]{:S(2)}) %collective-permute-start.1) | collective-permute-done | bytes 266272 | tf_op jit(solution)/shard_map/ppermute | solution.py:396
  14.0 0.0 copy-done.2
  14.0 1.9 %shard_map.97 = (bf16[16,64,128]{2,1,0:T(8,128)(2,1)S(1)}, bf16[512,128]{1,0:T(8,128)(2,1)S(1)}, bf16[512,128]{1,0:T(8,128)(2,1)S(1)}, bf16[512,128]{1,0:T(8,128)(2,1)S(1)}, f32[16,128]{1,0:T(8,128)S(1)}) custom-call(s32[16,128]{1,0:T(8,128)S(1)} %get-tuple-element.22.bases, bf16[1040,128]{1,0:T(8,128)(2,1)S(1)} %collective-permute-done.left, ...), custom_call_target="tpu_custom_call" | custom-call | tf_op jit(solution)/shard_map/pallas_call | solution.py:421
  15.9 2.3 %collective-permute-start.8 = (bf16[512,128]{1,0:T(8,128)(2,1)S(1)}, bf16[512,128]{1,0:T(8,128)(2,1)S(1)}, u32[]{:S(2)}, u32[]{:S(2)}) collective-permute-start(bf16[512,128]{1,0:T(8,128)(2,1)S(1)} %get-tuple-element.37), channel_id=1, source_target_pairs={{0,1},{1,0},{2,3},{3,2},{4,5},{5,4},{6,7},{7,6},{8,9},{9,8},{10,11... | collective-permute-start | bytes 393224 | tf_op jit(solution)/shard_map/ppermute | solution.py:434
  18.2 1.5 %shard_map.99 = (f32[16,64,128]{2,1,0:T(8,128)S(1)}, f32[16,64,128]{2,1,0:T(8,128)S(1)}) custom-call(s32[16,128]{1,0:T(8,128)S(1)} %bitcast.7, f32[32,128]{1,0:T(8,128)S(1)} %copy-done.4, f32[16,128]{1,0:T(8,128)S(1)} %copy-done.3, f32[2048,128]{1,0:T(8,128)S(1)} %copy-done), custom_call_target="tpu_custom_call" | custom-call | tf_op jit(solution)/shard_map/pallas_call | solution.py:401
  19.8 2.7 %collective-permute-start.4 = (bf16[512,128]{1,0:T(8,128)(2,1)S(1)}, bf16[512,128]{1,0:T(8,128)(2,1)S(1)}, u32[]{:S(2)}, u32[]{:S(2)}) collective-permute-start(bf16[512,128]{1,0:T(8,128)(2,1)S(1)} %get-tuple-element.33), channel_id=1, source_target_pairs={{0,2},{1,3},{2,0},{3,1},{4,6},{5,7},{6,4},{7,5},{8,10},{9,11},{10,... | collective-permute-start | bytes 393224 | tf_op jit(solution)/shard_map/ppermute | solution.py:434
  22.4 0.0 collective-permute-done.2.left
  22.4 0.0 collective-permute-done.3.right
  22.4 0.0 copy-start.1
  22.5 1.9 %shard_map.100 = (bf16[16,64,128]{2,1,0:T(8,128)(2,1)S(1)}, bf16[512,128]{1,0:T(8,128)(2,1)S(1)}, bf16[512,128]{1,0:T(8,128)(2,1)S(1)}, bf16[512,128]{1,0:T(8,128)(2,1)S(1)}) custom-call(s32[16,128]{1,0:T(8,128)S(1)} %get-tuple-element.22.bases, bf16[1024,128]{1,0:T(8,128)(2,1)S(1)} %collective-permute-done.2.left, ...), custom_call_target="tpu_custom_call" | custom-call | tf_op jit(solution)/shard_map/pallas_call | solution.py:421
  24.3 0.5 %collective-permute-start.9 = (bf16[512,128]{1,0:T(8,128)(2,1)S(1)}, bf16[512,128]{1,0:T(8,128)(2,1)S(1)}, u32[]{:S(2)}, u32[]{:S(2)}) collective-permute-start(bf16[512,128]{1,0:T(8,128)(2,1)S(1)} %get-tuple-element.38), channel_id=1, source_target_pairs={{0,1},{1,0},{2,3},{3,2},{4,5},{5,4},{6,7},{7,6},{8,9},{9,8},{10,11... | collective-permute-start | bytes 393224 | tf_op jit(solution)/shard_map/ppermute | solution.py:434
  24.9 1.4 %collective-permute-start.6 = (bf16[512,128]{1,0:T(8,128)(2,1)S(1)}, bf16[512,128]{1,0:T(8,128)(2,1)S(1)}, u32[]{:S(2)}, u32[]{:S(2)}) collective-permute-start(bf16[512,128]{1,0:T(8,128)(2,1)S(1)} %get-tuple-element.35), channel_id=1, source_target_pairs={{0,3},{1,2},{2,1},{3,0},{4,7},{5,6},{6,5},{7,4},{8,11},{9,10},{10,... | collective-permute-start | bytes 393224 | tf_op jit(solution)/shard_map/ppermute | solution.py:434
  26.2 2.5 %collective-permute-start.7 = (bf16[512,128]{1,0:T(8,128)(2,1)S(1)}, bf16[512,128]{1,0:T(8,128)(2,1)S(1)}, u32[]{:S(2)}, u32[]{:S(2)}) collective-permute-start(bf16[512,128]{1,0:T(8,128)(2,1)S(1)} %get-tuple-element.36), channel_id=1, source_target_pairs={{0,3},{1,2},{2,1},{3,0},{4,7},{5,6},{6,5},{7,4},{8,11},{9,10},{10,... | collective-permute-start | bytes 393224 | tf_op jit(solution)/shard_map/ppermute | solution.py:434
  28.7 0.0 collective-permute-done.8.refs_0_
  28.7 0.0 collective-permute-start.5
  28.7 0.0 copy-done.1
  28.7 4.4 %shard_map.101 = (bf16[2048,128]{1,0:T(8,128)(2,1)}, bf16[4,32,2,16,128]{4,3,2,1,0:T(8,128)(2,1)}) custom-call(s32[16,128]{1,0:T(8,128)S(1)} %get-tuple-element.22.bases, bf16[128,128]{1,0:T(8,128)(2,1)S(1)} %copy-done.1, f32[4,16,128]{2,1,0:T(8,128)S(1)} %get-tuple-element.23.keys, bf16[16,64,128]{2,1,0:T(8,128)(2,1)S(1)} %get-tuple-element.27.refs_0_, ...), custom_call_target="tpu_custom_call" | custom-call | tf_op jit(solution)/shard_map/pallas_call | solution.py:437
  33.2 4.5 %collective-permute-done.9.refs_1_ = bf16[512,128]{1,0:T(8,128)(2,1)S(1)} collective-permute-done((bf16[512,128]{1,0:T(8,128)(2,1)S(1)}, bf16[512,128]{1,0:T(8,128)(2,1)S(1)}, u32[]{:S(2)}, u32[]{:S(2)}) %collective-permute-start.9) | collective-permute-done | bytes 131104 | tf_op jit(solution)/shard_map/ppermute | solution.py:434
  37.7 2.4 %shard_map.102.refs_2_ = bf16[4,32,2,16,128]{4,3,2,1,0:T(8,128)(2,1)} custom-call(bf16[128,128]{1,0:T(8,128)(2,1)S(1)} %copy-done.1, bf16[512,128]{1,0:T(8,128)(2,1)S(1)} %collective-permute-done.8.refs_0_, bf16[512,128]{1,0:T(8,128)(2,1)S(1)} %collective-permute-done.9.refs_1_, ...), custom_call_target="tpu_custom_call", output_to_operand_aliasing={{}: (3, {})} | custom-call | tf_op jit(solution)/shard_map/pallas_call | solution.py:450
  40.1 0.0 collective-permute-done.6.refs_0_
  40.1 0.0 collective-permute-done.7.refs_1_
  40.1 2.4 %shard_map.103.refs_2_ = bf16[4,32,2,16,128]{4,3,2,1,0:T(8,128)(2,1)} custom-call(bf16[128,128]{1,0:T(8,128)(2,1)S(1)} %copy-done.1, bf16[512,128]{1,0:T(8,128)(2,1)S(1)} %collective-permute-done.6.refs_0_, bf16[512,128]{1,0:T(8,128)(2,1)S(1)} %collective-permute-done.7.refs_1_, ...), custom_call_target="tpu_custom_call", output_to_operand_aliasing={{}: (3, {})} | custom-call | tf_op jit(solution)/shard_map/pallas_call | solution.py:450
  42.6 0.0 collective-permute-done.4.refs_0_
  42.6 4.1 %collective-permute-done.5.refs_1_ = bf16[512,128]{1,0:T(8,128)(2,1)S(1)} collective-permute-done((bf16[512,128]{1,0:T(8,128)(2,1)S(1)}, bf16[512,128]{1,0:T(8,128)(2,1)S(1)}, u32[]{:S(2)}, u32[]{:S(2)}) %collective-permute-start.5) | collective-permute-done | bytes 131104 | tf_op jit(solution)/shard_map/ppermute | solution.py:434
  46.6 2.4 %shard_map.104 = bf16[4,32,2,16,128]{4,3,2,1,0:T(8,128)(2,1)} custom-call(bf16[128,128]{1,0:T(8,128)(2,1)S(1)} %copy-done.1, bf16[512,128]{1,0:T(8,128)(2,1)S(1)} %collective-permute-done.4.refs_0_, bf16[512,128]{1,0:T(8,128)(2,1)S(1)} %collective-permute-done.5.refs_1_, bf16[4,32,2,16,128]{4,3,2,1,0:T(8,128)(2,1)} %shard_map.103.refs_2_), custom_call_target="tpu_custom_call", output_to_operand_aliasing={{}: (3, {})} | custom-call | tf_op jit(solution)/shard_map/pallas_call | solution.py:450
Async XLA Ops:
  0.6 6.3 %copy-start = (f32[2048,128]{1,0:T(8,128)S(1)}, f32[2048,128]{1,0:T(8,128)}, u32[]{:S(2)}) copy-start(f32[2048,128]{1,0:T(8,128)} %conc.7) | copy-start | bytes 3145732
  3.4 8.8 %collective-permute-start = (bf16[1040,128]{1,0:T(8,128)(2,1)}, bf16[1040,128]{1,0:T(8,128)(2,1)S(1)}, u32[]{:S(2)}, u32[]{:S(2)}) collective-permute-start(bf16[1040,128]{1,0:T(8,128)(2,1)} %get-tuple-element.24.high), channel_id=1, source_target_pairs={{0,4},{4,8},{8,12},{12,16},{16,20},{20,24},{24,28},{28,0},{1,5},{5... | collective-permute-start | bytes 798728 | tf_op jit(solution)/shard_map/ppermute | solution.py:395
  4.0 10.0 %collective-permute-start.1 = (bf16[1040,128]{1,0:T(8,128)(2,1)}, bf16[1040,128]{1,0:T(8,128)(2,1)S(1)}, u32[]{:S(2)}, u32[]{:S(2)}) collective-permute-start(bf16[1040,128]{1,0:T(8,128)(2,1)} %get-tuple-element.24.high), channel_id=1, source_target_pairs={{4,0},{8,4},{12,8},{16,12},{20,16},{24,20},{28,24},{0,28},{5,1},{9... | collective-permute-start | bytes 798728 | tf_op jit(solution)/shard_map/ppermute | solution.py:396
  6.9 3.6 %copy-start.3 = (f32[16,128]{1,0:T(8,128)S(1)}, f32[16,128]{1,0:T(8,128)}, u32[]{:S(2)}) copy-start(f32[16,128]{1,0:T(8,128)} %get-tuple-element.21.table) | copy-start | bytes 24580
  6.9 3.6 %copy-start.4 = (f32[32,128]{1,0:T(8,128)S(1)}, f32[32,128]{1,0:T(8,128)}, u32[]{:S(2)}) copy-start(f32[32,128]{1,0:T(8,128)} %rates.3) | copy-start | bytes 49156
  6.9 3.6 %copy-start.5 = (s32[2048]{0:T(1024)S(1)}, s32[2048]{0:T(1024)}, u32[]{:S(2)}) copy-start(s32[2048]{0:T(1024)} %param.12) | copy-start | bytes 24580
  6.9 3.6 %copy-start.6 = (s32[2048,1]{0,1:T(1,128)S(1)}, s32[2048,1]{0,1:T(1,128)}, u32[]{:S(2)}) copy-start(s32[2048,1]{0,1:T(1,128)} %param.13) | copy-start | bytes 24580
  7.8 14.7 %collective-permute-start.2 = (bf16[1024,128]{1,0:T(8,128)(2,1)S(1)}, bf16[1024,128]{1,0:T(8,128)(2,1)S(1)}, u32[]{:S(2)}, u32[]{:S(2)}) collective-permute-start(bf16[1024,128]{1,0:T(8,128)(2,1)S(1)} %shard_map.98.high), channel_id=1, source_target_pairs={{0,4},{4,8},{8,12},{12,16},{16,20},{20,24},{24,28},{28,0},{1,5},{5... | collective-permute-start | bytes 786440 | tf_op jit(solution)/shard_map/ppermute | solution.py:395
  7.9 14.6 %collective-permute-start.3 = (bf16[1024,128]{1,0:T(8,128)(2,1)S(1)}, bf16[1024,128]{1,0:T(8,128)(2,1)S(1)}, u32[]{:S(2)}, u32[]{:S(2)}) collective-permute-start(bf16[1024,128]{1,0:T(8,128)(2,1)S(1)} %shard_map.98.high), channel_id=1, source_target_pairs={{4,0},{8,4},{12,8},{16,12},{20,16},{24,20},{28,24},{0,28},{5,1},{9... | collective-permute-start | bytes 786440 | tf_op jit(solution)/shard_map/ppermute | solution.py:396
  10.5 3.5 %copy-start.2 = (bf16[1040,128]{1,0:T(8,128)(2,1)S(1)}, bf16[1040,128]{1,0:T(8,128)(2,1)}, u32[]{:S(2)}) copy-start(bf16[1040,128]{1,0:T(8,128)(2,1)} %get-tuple-element.24.high) | copy-start | bytes 798724
  15.9 12.8 %collective-permute-start.8 = (bf16[512,128]{1,0:T(8,128)(2,1)S(1)}, bf16[512,128]{1,0:T(8,128)(2,1)S(1)}, u32[]{:S(2)}, u32[]{:S(2)}) collective-permute-start(bf16[512,128]{1,0:T(8,128)(2,1)S(1)} %get-tuple-element.37), channel_id=1, source_target_pairs={{0,1},{1,0},{2,3},{3,2},{4,5},{5,4},{6,7},{7,6},{8,9},{9,8},{10,11... | collective-permute-start | bytes 393224 | tf_op jit(solution)/shard_map/ppermute | solution.py:434
  19.8 22.8 %collective-permute-start.4 = (bf16[512,128]{1,0:T(8,128)(2,1)S(1)}, bf16[512,128]{1,0:T(8,128)(2,1)S(1)}, u32[]{:S(2)}, u32[]{:S(2)}) collective-permute-start(bf16[512,128]{1,0:T(8,128)(2,1)S(1)} %get-tuple-element.33), channel_id=1, source_target_pairs={{0,2},{1,3},{2,0},{3,1},{4,6},{5,7},{6,4},{7,5},{8,10},{9,11},{10,... | collective-permute-start | bytes 393224 | tf_op jit(solution)/shard_map/ppermute | solution.py:434
  22.4 6.2 %copy-start.1 = (bf16[128,128]{1,0:T(8,128)(2,1)S(1)}, bf16[128,128]{1,0:T(8,128)(2,1)}, u32[]{:S(2)}) copy-start(bf16[128,128]{1,0:T(8,128)(2,1)} %reaction.7) | copy-start | bytes 98308
  24.3 13.4 %collective-permute-start.9 = (bf16[512,128]{1,0:T(8,128)(2,1)S(1)}, bf16[512,128]{1,0:T(8,128)(2,1)S(1)}, u32[]{:S(2)}, u32[]{:S(2)}) collective-permute-start(bf16[512,128]{1,0:T(8,128)(2,1)S(1)} %get-tuple-element.38), channel_id=1, source_target_pairs={{0,1},{1,0},{2,3},{3,2},{4,5},{5,4},{6,7},{7,6},{8,9},{9,8},{10,11... | collective-permute-start | bytes 393224 | tf_op jit(solution)/shard_map/ppermute | solution.py:434
  24.9 15.3 %collective-permute-start.6 = (bf16[512,128]{1,0:T(8,128)(2,1)S(1)}, bf16[512,128]{1,0:T(8,128)(2,1)S(1)}, u32[]{:S(2)}, u32[]{:S(2)}) collective-permute-start(bf16[512,128]{1,0:T(8,128)(2,1)S(1)} %get-tuple-element.35), channel_id=1, source_target_pairs={{0,3},{1,2},{2,1},{3,0},{4,7},{5,6},{6,5},{7,4},{8,11},{9,10},{10,... | collective-permute-start | bytes 393224 | tf_op jit(solution)/shard_map/ppermute | solution.py:434
  26.2 13.9 %collective-permute-start.7 = (bf16[512,128]{1,0:T(8,128)(2,1)S(1)}, bf16[512,128]{1,0:T(8,128)(2,1)S(1)}, u32[]{:S(2)}, u32[]{:S(2)}) collective-permute-start(bf16[512,128]{1,0:T(8,128)(2,1)S(1)} %get-tuple-element.36), channel_id=1, source_target_pairs={{0,3},{1,2},{2,1},{3,0},{4,7},{5,6},{6,5},{7,4},{8,11},{9,10},{10,... | collective-permute-start | bytes 393224 | tf_op jit(solution)/shard_map/ppermute | solution.py:434
  28.7 18.0 %collective-permute-start.5 = (bf16[512,128]{1,0:T(8,128)(2,1)S(1)}, bf16[512,128]{1,0:T(8,128)(2,1)S(1)}, u32[]{:S(2)}, u32[]{:S(2)}) collective-permute-start(bf16[512,128]{1,0:T(8,128)(2,1)S(1)} %get-tuple-element.34), channel_id=1, source_target_pairs={{0,2},{1,3},{2,0},{3,1},{4,6},{5,7},{6,4},{7,5},{8,10},{9,11},{10,... | collective-permute-start | bytes 393224 | tf_op jit(solution)/shard_map/ppermute | solution.py:434

commit v2 on v1

--- a/solution.py
+++ b/solution.py
@@ -17,11 +17,11 @@
 CHUNKS = 2
 LOADS = 4
 TILES = 4
+LATE = 4
 
 F32 = jnp.float32
 BF16 = jnp.bfloat16
 VMEM = pl.BlockSpec(memory_space=pltpu.VMEM)
-SMEM = pl.BlockSpec(memory_space=pltpu.SMEM)
 ANY = pl.BlockSpec(memory_space=pl.ANY)
 HBM = pl.BlockSpec(memory_space=pltpu.HBM)
 
@@ -71,31 +71,19 @@
 
 def pack_kernel(chunks, chunk, nblocks, conc, *refs):
     span = BLK // chunks
+    loads, stage = [], conc
     if chunk == 0:
-        lists, msg, table, held = refs[:3], refs[3], refs[4], refs[5:8]
-        stage, buffer, sems = refs[8:]
+        lists, msg, table, stage, held, sems = refs[:3], *refs[3:6], refs[6:9], refs[9]
         small = [
-            pltpu.make_async_copy(source, target, sems.at[2 * LOADS + 1 + i])
+            pltpu.make_async_copy(source, target, sems.at[LOADS + i])
             for i, (source, target) in enumerate(zip(lists, held))
         ]
         for copy in small:
             copy.start()
-        neighbours, counts, weights = held
-    else:
-        msg, stage, buffer, sems = refs
-    loads = load_all(conc, stage, sems)
-    stores = []
-
-    def store(i, first, rows):
-        copy = pltpu.make_async_copy(
-            buffer.at[pl.ds(first, rows)], msg.at[pl.ds(first, rows)], sems.at[LOADS + i]
-        )
-        copy.start()
-        stores.append(copy)
-
-    if chunk == 0:
+        loads = load_all(conc, stage, sems)
         for copy in small:
             copy.wait()
+        neighbours, counts, weights = held
         nlon, nbal = lax.axis_size("lon"), lax.axis_size("bal")
         me = lax.axis_index("lon") * nbal + lax.axis_index("bal")
         column = iota((3 * nblocks, nblocks), 0)
@@ -114,17 +102,16 @@
         table[...] = dot_first(pairs, eye(3 * nblocks)) + dot(pairs[:nblocks], eye(nblocks))
         carried = dot(pairs[2 * nblocks :], eye(nblocks, nblocks))
         carried = carried + dot(pairs[nblocks : 2 * nblocks], eye(nblocks, 2 * nblocks))
-        buffer[nblocks * span :, :] = carried.astype(BF16)
-        store(LOADS, nblocks * span, nblocks)
+        msg[nblocks * span :, :] = carried.astype(BF16)
+    else:
+        (msg,) = refs
     each = nblocks // LOADS
-    for i in range(LOADS):
-        loads[i].wait()
-        for b in range(i * each, (i + 1) * each):
-            rows = [stage[b * BLK + j * span : b * BLK + (j + 1) * span, :] for j in range(chunks)]
-            buffer[b * span : (b + 1) * span, :] = regroup(rows, chunk, chunks).astype(BF16)
-        store(i, i * each * span, each * span)
-    for copy in stores:
-        copy.wait()
+    for b in range(nblocks):
+        if loads and b % each == 0:
+            loads[b // each].wait()
+        rows = [stage[b * BLK + j * span : b * BLK + (j + 1) * span, :] for j in range(chunks)]
+        rows = [row.astype(BF16) for row in rows]
+        msg[b * span : (b + 1) * span, :] = regroup(rows, chunk, chunks)
 
 
 def tall(value, rows):
@@ -160,10 +147,9 @@
 def prepare_kernel(chunks, chunk, nblocks, nbal, zones, rates, table, conc, *refs):
     span, width = BLK // chunks, LANES // chunks
     if chunk == 0:
-        owners, factor, kept, keys, bases, stage, value, sems = refs
+        owners, factor, kept, keys, bases, value = refs
     else:
-        factor, kept, stage, value, sems = refs
-    loads = load_all(conc, stage, sems)
+        factor, kept, value = refs
 
     decay = jnp.exp(-rates[...])
     lane = iota((span, LANES), 1)
@@ -211,12 +197,9 @@
     lane = iota((nblocks, LANES), 1)
     inner = jnp.sum(jnp.where(lane < nblocks, coupling, 0.0), axis=1, keepdims=True)
     keep = tall(1.0 - inner, TILE)
-    each = nblocks // LOADS
-    for i in range(LOADS):
-        loads[i].wait()
-        for b in range(i * each, (i + 1) * each):
-            rows = [stage[b * BLK + j * span : b * BLK + (j + 1) * span, :] for j in range(chunks)]
-            value[b * span : (b + 1) * span, :] = regroup(rows, chunk, chunks)
+    for b in range(nblocks):
+        rows = [conc[b * BLK + j * span : b * BLK + (j + 1) * span, :] for j in range(chunks)]
+        value[b * span : (b + 1) * span, :] = regroup(rows, chunk, chunks)
     for u in range(0, span // TILE, 2):
         whole = pieces(value, u, nblocks, span)
         high = whole.astype(BF16)
@@ -233,7 +216,9 @@
     span, width = BLK // chunks, LANES // chunks
     rows = nblocks * span
     start, slots = refs[0], refs[1:nbal]
-    buffer = refs[-1]
+    buffer, places, sem = refs[-3:]
+    copy = pltpu.make_async_copy(bases, places, sem)
+    copy.start()
     lane = iota((nblocks, LANES), 1)
     coupling = table[...]
     if chunk == 0:
@@ -268,13 +253,13 @@
         for jj in range(chunks)
     ]
     group = lax.shift_right_logical(iota((reach, LANES), 1), width.bit_length() - 1)
+    copy.wait()
     for b in range(nblocks):
         select = []
         for k in range(1, nbal):
             key = jnp.broadcast_to(keys[k, b : b + 1, :], (reach, LANES))
             select += [jnp.where(key == m, 1.0, 0.0).astype(BF16) for m in marks]
-        block = start[b].astype(F32)
-        spread = [regroup([block] * chunks, j, chunks).astype(BF16) for j in range(chunks)]
+        spread = [regroup([start[b]] * chunks, j, chunks) for j in range(chunks)]
         placed = dot(jnp.concatenate(select, axis=0), jnp.concatenate(spread, axis=0))
         for k in range(1, nbal):
             first = (k - 1) * chunks * reach
@@ -283,7 +268,7 @@
                 other = placed[first + jj * reach : first + (jj + 1) * reach]
                 window = jnp.where(group == jj, other, window)
             window = window.astype(BF16)
-            at = pl.multiple_of(bases[b, k], TILE)
+            at = pl.multiple_of(jnp.minimum(places[b, k], depth), TILE)
             buffer[k - 1, pl.ds(at, TILE), :] = buffer[k - 1, pl.ds(at, TILE), :] + window[:TILE]
             buffer[k - 1, pl.ds(at + TILE, span), :] = window[TILE:]
     for k in range(1, nbal):
@@ -300,56 +285,95 @@
             state[t * rows : (t + 1) * rows, :] = current + jnp.tanh(tendency)
 
 
-def own_kernel(chunks, nblocks, bases, reaction, keys, *refs):
-    starts, out, slots, state, done, buffer, sem = refs[:chunks], *refs[chunks:]
-    span = BLK // chunks
+def own_kernel(chunks, nblocks, nbal, bases, reaction, keys, *refs):
+    starts, out, slots, lates = refs[:chunks], refs[chunks], refs[chunks + 1], refs[chunks + 2 : -6]
+    state, done, mine, others, places, sems = refs[-6:]
+    copy = pltpu.make_async_copy(bases, places, sems.at[2])
+    copy.start()
+    span, capacity, late = BLK // chunks, slots.shape[1], lates[0].shape[0]
     for b in range(nblocks):
-        rows = [starts[c][b].astype(F32) * 4.0 for c in range(chunks)]
         for j in range(chunks):
             first = b * BLK + j * span
-            state[first : first + span, :] = regroup(rows, j, chunks)
+            rows = regroup([starts[c][b] for c in range(chunks)], j, chunks)
+            state[first : first + span, :] = rows.astype(F32) * 4.0
     chemistry(state, reaction)
     done[...] = (state[...] * 0.25).astype(BF16)
-    out[...] = done[...]
-    reach = BLK + TILE * chunks
-    capacity = slots.shape[1] * slots.shape[2] * slots.shape[3]
-    buffer[...] = jnp.zeros(buffer.shape, BF16)
+    result = pltpu.make_async_copy(done, out, sems.at[0])
+    result.start()
+    edge = TILE * chunks
+    reach = BLK + edge
+    mine[...] = jnp.zeros(mine.shape, BF16)
+    others[...] = jnp.zeros(others.shape, BF16)
     mark = iota((reach, LANES), 0).astype(F32)
+    copy.wait()
     for b in range(nblocks):
-        key = jnp.broadcast_to(keys[0, b : b + 1, :], (reach, LANES))
-        select = jnp.where(key == mark, 1.0, 0.0).astype(BF16)
-        window = dot(select, done[b * BLK : (b + 1) * BLK, :]).astype(BF16)
-        at = pl.multiple_of(bases[b, 0] * chunks, TILE)
-        edge = TILE * chunks
-        buffer[pl.ds(at, edge), :] = buffer[pl.ds(at, edge), :] + window[:edge]
-        buffer[pl.ds(at + edge, BLK), :] = window[edge:]
-    for _ in range(1):
-        copy = pltpu.make_async_copy(
-            buffer.at[pl.ds(0, capacity)].reshape(slots.shape[1:]), slots.at[lax.axis_index("bal")], sem
+        select = []
+        for k in range(nbal):
+            key = jnp.broadcast_to(keys[k, b : b + 1, :], (reach, LANES))
+            select.append(jnp.where(key == mark, 1.0, 0.0).astype(BF16))
+        placed = dot(jnp.concatenate(select, axis=0), done[b * BLK : (b + 1) * BLK, :]).astype(BF16)
+        for k in range(nbal):
+            at = places[b, k] * chunks
+            target = mine
+            if k:
+                at = jnp.maximum(at - (capacity - late - reach), 0)
+                target = others.at[k - 1]
+            at = pl.multiple_of(at, TILE)
+            window = placed[k * reach : (k + 1) * reach]
+            target[pl.ds(at, edge), :] = target[pl.ds(at, edge), :] + window[:edge]
+            target[pl.ds(at + edge, BLK), :] = window[edge:]
+    own = pltpu.make_async_copy(
+        mine.at[pl.ds(0, capacity)], slots.at[lax.axis_index("bal")], sems.at[1]
+    )
+    own.start()
+    for k in range(1, nbal):
+        lates[k - 1][...] = others[k - 1, reach : reach + late, :]
+    result.wait()
+    own.wait()
+
+
+def slot_kernel(chunks, nbal, reaction, *refs):
+    parts = refs[: (nbal - 1) * chunks]
+    out, state, result, sems = refs[-4:]
+    depth = parts[0].shape[0]
+    early = depth * chunks
+    for k in range(1, nbal):
+        mine = parts[(k - 1) * chunks : k * chunks]
+        for jj in range(chunks):
+            first = (k - 1) * early + jj * depth
+            rows = regroup([part[...] for part in mine], jj, chunks)
+            state[first : first + depth, :] = rows.astype(F32) * 4.0
+    chemistry(state, reaction)
+    copies = []
+    for k in range(1, nbal):
+        for jj in range(chunks):
+            first = (k - 1) * early + jj * depth
+            done = (state[first : first + depth, :] * 0.25).astype(BF16)
+            result[k - 1, :, jj] = done.reshape(depth // TILE, TILE, LANES)
+        place = jnp.bitwise_xor(lax.axis_index("bal"), k)
+        copies.append(
+            pltpu.make_async_copy(
+                result.at[k - 1].reshape(early, LANES),
+                out.at[place, pl.ds(0, early)],
+                sems.at[k - 1],
+            )
         )
-        copy.start()
+        copies[-1].start()
+    for copy in copies:
         copy.wait()
 
 
-def slot_kernel(chunks, k, reaction, *refs):
-    parts = refs[:chunks]
-    out, state, result, sem = refs[-4:]
-    depth = parts[0].shape[0]
-    rows = [part[...].astype(F32) * 4.0 for part in parts]
-    for jj in range(chunks):
-        state[jj * depth : (jj + 1) * depth, :] = regroup(rows, jj, chunks)
-    chemistry(state, reaction)
-    for jj in range(chunks):
-        done = (state[jj * depth : (jj + 1) * depth, :] * 0.25).astype(BF16)
-        result[:, jj] = done.reshape(depth // TILE, TILE, LANES)
-    place = jnp.bitwise_xor(lax.axis_index("bal"), k)
-    copy = pltpu.make_async_copy(result, out.at[place], sem)
-    copy.start()
-    copy.wait()
-
-
-def ORDER(nbal):
-    return [k for k in range(1, nbal) if k != 2] + [2]
+def late_kernel(nbal, *refs):
+    lates, out, sems = refs[: nbal - 1], refs[-2], refs[-1]
+    late = lates[0].shape[0]
+    copies = []
+    for k in range(1, nbal):
+        place = jnp.bitwise_xor(lax.axis_index("bal"), k)
+        target = out.at[place, pl.ds(out.shape[1] - late, late)]
+        copies.append(pltpu.make_async_copy(lates[k - 1], target, sems.at[k - 1]))
+        copies[-1].start()
+    for copy in copies:
+        copy.wait()
 
 
 def step(conc, neighbours, counts, weights, zones, owners, rate_table, reaction):
@@ -359,15 +383,19 @@
     chunks = CHUNKS
     span = BLK // chunks
     capacity = 2 * rows // nbal
-    depth = capacity // chunks
+    late = capacity // LATE
+    depth = (capacity - late) // chunks
 
     shape = jax.ShapeDtypeStruct
     zones, owners = zones.reshape(nblocks, BLK), owners.reshape(nblocks, BLK)
     blocked = shape((nblocks, span, LANES), F32)
 
-    def call(body, limit=16, **kw):
-        params = pltpu.CompilerParams(vmem_limit_bytes=limit << 20)
+    def call(body, **kw):
+        params = pltpu.CompilerParams(vmem_limit_bytes=16 << 20)
         return pl.pallas_call(body, compiler_params=params, **kw)
+
+    def in_hbm(array):
+        return pltpu.with_memory_space_constraint(array, pltpu.HBM)
 
     ahead = [(i, (i + 1) % nlon) for i in range(nlon)]
     back = [((i + 1) % nlon, i) for i in range(nlon)]
@@ -378,19 +406,15 @@
         length = nblocks * span + (nblocks if first else 0)
         outs = call(
             functools.partial(pack_kernel, chunks, c, nblocks),
-            60 if first else 16,
-            out_shape=[shape((length, LANES), BF16)] + [shape((nblocks, LANES), F32)] * first,
-            in_specs=[HBM] * (1 + 3 * first),
-            out_specs=[ANY] + [VMEM] * first,
+            out_shape=[shape((length, LANES), BF16)]
+            + [shape((nblocks, LANES), F32), shape((rows, LANES), F32)] * first,
+            in_specs=[HBM] * 4 if first else [VMEM],
+            out_specs=[VMEM] * (1 + 2 * first),
             scratch_shapes=[pltpu.VMEM(a.shape, jnp.int32) for a in lists if first]
-            + [
-                pltpu.VMEM((rows, LANES), F32),
-                pltpu.VMEM((length, LANES), BF16),
-                pltpu.SemaphoreType.DMA((2 * LOADS + 4,)),
-            ],
-        )(conc, *(lists if first else ()))
+            + [pltpu.SemaphoreType.DMA((LOADS + 3,))] * first,
+        )(*((in_hbm(conc), *map(in_hbm, lists)) if first else (stage,)))
         if first:
-            table = outs[1]
+            table, stage = outs[1:]
         msgs.append(outs[0])
         lefts.append(lax.ppermute(outs[0], "lon", ahead))
         rights.append(lax.ppermute(outs[0], "lon", back))
@@ -402,14 +426,10 @@
             functools.partial(prepare_kernel, chunks, c, nblocks, nbal),
             out_shape=[blocked, blocked]
             + [shape((nbal, nblocks, LANES), F32), shape((nblocks, LANES), jnp.int32)] * first,
-            in_specs=[VMEM] * 3 + [HBM] + [VMEM] * first,
+            in_specs=[VMEM] * (4 + first),
             out_specs=[VMEM] * (2 + 2 * first),
-            scratch_shapes=[
-                pltpu.VMEM((rows, LANES), F32),
-                pltpu.VMEM((nblocks * span, LANES), F32),
-                pltpu.SemaphoreType.DMA((LOADS,)),
-            ],
-        )(zones, rate_table, table, conc, *([owners] if first else []))
+            scratch_shapes=[pltpu.VMEM((nblocks * span, LANES), F32)],
+        )(zones, rate_table, table, stage, *([owners] if first else []))
         factors.append(outs[0])
         kepts.append(outs[1])
         if first:
@@ -423,9 +443,13 @@
             out_shape=[shape((nblocks, span, LANES), BF16)]
             + [shape((depth, LANES), BF16)] * (nbal - 1)
             + [shape((nblocks, LANES), F32)] * first,
-            in_specs=[SMEM] + [VMEM] * 7,
+            in_specs=[VMEM] * 8,
             out_specs=[VMEM] * (nbal + first),
-            scratch_shapes=[pltpu.VMEM((nbal - 1, depth + span + TILE, LANES), BF16)],
+            scratch_shapes=[
+                pltpu.VMEM((nbal - 1, depth + span + TILE, LANES), BF16),
+                pltpu.SMEM(bases.shape, jnp.int32),
+                pltpu.SemaphoreType.DMA,
+            ],
         )(bases, lefts[c], rights[c], table, msgs[c], kepts[c], factors[c], keys)
         starts.append(outs[0])
         if first:
@@ -433,32 +457,45 @@
         for k in range(1, nbal):
             received[k][c] = lax.ppermute(outs[k], "bal", [(i, i ^ k) for i in range(nbal)])
 
-    tiles = shape((nbal, depth // TILE, chunks, TILE, LANES), BF16)
-    conc_out, chem = call(
-        functools.partial(own_kernel, chunks, nblocks),
-        out_shape=[shape((rows, LANES), BF16), tiles],
-        in_specs=[SMEM] + [VMEM] * (2 + chunks),
-        out_specs=[VMEM, ANY],
+    slots = shape((nbal, capacity, LANES), BF16)
+    reach = BLK + TILE * chunks
+    conc_out, chem, *lates = call(
+        functools.partial(own_kernel, chunks, nblocks, nbal),
+        out_shape=[shape((rows, LANES), BF16), slots] + [shape((late, LANES), BF16)] * (nbal - 1),
+        in_specs=[VMEM] * (3 + chunks),
+        out_specs=[ANY, ANY] + [VMEM] * (nbal - 1),
         scratch_shapes=[
             pltpu.VMEM((rows, LANES), F32),
             pltpu.VMEM((rows, LANES), BF16),
-            pltpu.VMEM((capacity + BLK + TILE * chunks, LANES), BF16),
-            pltpu.SemaphoreType.DMA,
+            pltpu.VMEM((capacity + reach, LANES), BF16),
+            pltpu.VMEM((nbal - 1, late + 2 * reach, LANES), BF16),
+            pltpu.SMEM(bases.shape, jnp.int32),
+            pltpu.SemaphoreType.DMA((3,)),
         ],
     )(bases, reaction, keys, *starts)
-    for k in ORDER(nbal):
-        chem = call(
-            functools.partial(slot_kernel, chunks, k),
-            out_shape=tiles,
-            in_specs=[VMEM] * (1 + chunks) + [ANY],
-            out_specs=ANY,
-            scratch_shapes=[
-                pltpu.VMEM((capacity, LANES), F32),
-                pltpu.VMEM(tiles.shape[1:], BF16),
-                pltpu.SemaphoreType.DMA,
-            ],
-            input_output_aliases={1 + chunks: 0},
-        )(reaction, *received[k], chem)
+    for k in range(1, nbal):
+        moved = lax.ppermute(lates[k - 1], "bal", [(i, i ^ k) for i in range(nbal)])
+        lates[k - 1] = moved
+    chem = call(
+        functools.partial(slot_kernel, chunks, nbal),
+        out_shape=slots,
+        in_specs=[VMEM] * (1 + chunks * (nbal - 1)) + [ANY],
+        out_specs=ANY,
+        scratch_shapes=[
+            pltpu.VMEM(((nbal - 1) * (capacity - late), LANES), F32),
+            pltpu.VMEM((nbal - 1, depth // TILE, chunks, TILE, LANES), BF16),
+            pltpu.SemaphoreType.DMA((nbal - 1,)),
+        ],
+        input_output_aliases={1 + chunks * (nbal - 1): 0},
+    )(reaction, *[part for group in received[1:] for part in group], chem)
+    chem = call(
+        functools.partial(late_kernel, nbal),
+        out_shape=slots,
+        in_specs=[VMEM] * (nbal - 1) + [ANY],
+        out_specs=ANY,
+        scratch_shapes=[pltpu.SemaphoreType.DMA((nbal - 1,))],
+        input_output_aliases={nbal - 1: 0},
+    )(*lates, chem)
     return conc_out, chem.reshape(nbal * capacity, width)
 
 

time: 49.2 us -> 46 us (0.935)
  Pallas kernels: 22.3 us -> 13.6 us
  starting transfers between devices: 15.5 us -> 23.9 us
  waiting for transfers between devices: 10.5 us -> 7.5 us
    ppermute x0 -> x3, starting transfers between devices: none -> 9.49 us  [step(): moved = lax.ppermute(lates[k - 1], 'bal', [(i, i ^ k) for i in range(nbal)])]
    ppermute x6, waiting for transfers between devices: 8.63 us -> 0.4 us  [step(): lax.ppermute(outs[k], 'bal', [(i, i ^ k) for i in range(nbal)])]
    pallas_call x6 -> x5, Pallas kernels: 15.3 us -> 8.5 us  [the longest x1 3.42 us: step(): call(functools.partial(own_kernel, chunks, nblocks, nbal), out_shape=[sha...]
    ppermute x0 -> x3, waiting for transfers between devices: none -> 2.18 us  [step(): moved = lax.ppermute(lates[k - 1], 'bal', [(i, i ^ k) for i in range(nbal)])]
    ppermute x2, waiting for transfers between devices: 0.01 us -> 1.59 us  [step(): lefts.append(lax.ppermute(outs[0], 'lon', ahead))]
    ppermute x2, waiting for transfers between devices: 1.82 us -> 3.34 us  [step(): rights.append(lax.ppermute(outs[0], 'lon', back))]
    pallas_call x2, Pallas kernels: 3.18 us -> 2.02 us  [step(): call(functools.partial(prepare_kernel, chunks, c, nblocks, nbal), out_sha...]
    ppermute x6, starting transfers between devices: 9.33 us -> 8.29 us  [step(): lax.ppermute(outs[k], 'bal', [(i, i ^ k) for i in range(nbal)])]
  transfers between devices with their start and end apart: 10 -> 13, of which waited for: 3 -> 5; matrix products, arithmetic and copies ran while one was open for 0% -> 0% of each run, Pallas kernels for 35% -> 22%
where the time goes in v2:
time: 46 us; the launch traced here: 45.8 us
  starting transfers between devices  23.9 us (52%)
  Pallas kernels  13.6 us (30%)
  waiting for transfers between devices  7.5 us (16%)
  between operations  0.75 us (2%)
    ppermute x3, starting transfers between devices, step(): moved = lax.ppermute(lates[k - 1], 'bal', [(i, i ^ k) for i in range(nbal)])  9.49 us
    ppermute x6, starting transfers between devices, step(): lax.ppermute(outs[k], 'bal', [(i, i ^ k) for i in range(nbal)])  8.29 us
    ppermute x2, starting transfers between devices, step(): rights.append(lax.ppermute(outs[0], 'lon', back))  5.57 us
    pallas_call x1, Pallas kernels, step(): call(functools.partial(own_kernel, chunks, nblocks, nbal), out_shape=[sha...  3.42 us
    ppermute x2, waiting for transfers between devices, step(): rights.append(lax.ppermute(outs[0], 'lon', back))  3.34 us
    pallas_call x2, Pallas kernels, step(): call(functools.partial(mix_kernel, chunks, c, nblocks, nbal), out_shape=[...  3.06 us
    pallas_call x1, Pallas kernels, step(): call(functools.partial(slot_kernel, chunks, nbal), out_shape=slots, in_sp...  2.85 us
    ppermute x3, waiting for transfers between devices, step(): moved = lax.ppermute(lates[k - 1], 'bal', [(i, i ^ k) for i in range(nbal)])  2.18 us
  transfers between devices with their start and end apart: 13, of which 5 were waited for; matrix products, arithmetic and copies ran while one was open for 0% of the time, Pallas kernels for 22%

profile of v2, /device:TPU:0, one launch (start us, length us, event | category | flops | bytes accessed | tf_op | source)
XLA Modules:
  0.0 45.8 jit_solution(11205762011404478242)
XLA Ops:
  0.6 1.4 %shard_map.95 = (bf16[1040,128]{1,0:T(8,128)(2,1)S(1)}, f32[16,128]{1,0:T(8,128)S(1)}, f32[2048,128]{1,0:T(8,128)S(1)}) custom-call(f32[2048,128]{1,0:T(8,128)} %conc.1, s32[8,16]{1,0:T(8,128)} %bitcast.10, s32[1,16]{1,0:T(1,128)} %bitcast.12, s32[8,16]{1,0:T(8,128)} %bitcast.11), custom_call_target="tpu_custom_call" | custom-call | tf_op jit(solution)/shard_map/pallas_call | solution.py:407
  2.0 0.5 %collective-permute-start = (bf16[1040,128]{1,0:T(8,128)(2,1)S(1)}, bf16[1040,128]{1,0:T(8,128)(2,1)S(1)}, u32[]{:S(2)}, u32[]{:S(2)}) collective-permute-start(bf16[1040,128]{1,0:T(8,128)(2,1)S(1)} %get-tuple-element.29.high), channel_id=1, source_target_pairs={{0,4},{4,8},{8,12},{12,16},{16,20},{20,24},{24,28},{28,0},{1,5},{5... | collective-permute-start | bytes 798728 | tf_op jit(solution)/shard_map/ppermute | solution.py:419
  2.6 2.9 %collective-permute-start.1 = (bf16[1040,128]{1,0:T(8,128)(2,1)S(1)}, bf16[1040,128]{1,0:T(8,128)(2,1)S(1)}, u32[]{:S(2)}, u32[]{:S(2)}) collective-permute-start(bf16[1040,128]{1,0:T(8,128)(2,1)S(1)} %get-tuple-element.29.high), channel_id=1, source_target_pairs={{4,0},{8,4},{12,8},{16,12},{20,16},{24,20},{28,24},{0,28},{5,1},{9... | collective-permute-start | bytes 798728 | tf_op jit(solution)/shard_map/ppermute | solution.py:420
  5.5 0.0 copy-start.1
  5.5 0.0 copy-start.2
  5.5 0.1 shard_map.98.high
  5.7 0.1 collective-permute-start.2
  5.7 2.6 %collective-permute-start.3 = (bf16[1024,128]{1,0:T(8,128)(2,1)S(1)}, bf16[1024,128]{1,0:T(8,128)(2,1)S(1)}, u32[]{:S(2)}, u32[]{:S(2)}) collective-permute-start(bf16[1024,128]{1,0:T(8,128)(2,1)S(1)} %shard_map.98.high), channel_id=1, source_target_pairs={{4,0},{8,4},{12,8},{16,12},{20,16},{24,20},{28,24},{0,28},{5,1},{9... | collective-permute-start | bytes 786440 | tf_op jit(solution)/shard_map/ppermute | solution.py:420
  8.4 0.0 copy-done.1
  8.4 0.0 copy-done.2
  8.4 0.0 copy-start.3
  8.4 1.0 %shard_map.99 = (f32[16,64,128]{2,1,0:T(8,128)S(1)}, f32[16,64,128]{2,1,0:T(8,128)S(1)}) custom-call(s32[16,128]{1,0:T(8,128)S(1)} %bitcast.6, f32[32,128]{1,0:T(8,128)S(1)} %copy-done.1, f32[16,128]{1,0:T(8,128)S(1)} %get-tuple-element.25.table, f32[2048,128]{1,0:T(8,128)S(1)} %get-tuple-element.26.conc), custom_call_target="tpu_custom_call" | custom-call | tf_op jit(solution)/shard_map/pallas_call | solution.py:425
  9.4 0.0 copy-done.3
  9.4 1.0 %shard_map.96 = (f32[16,64,128]{2,1,0:T(8,128)S(1)}, f32[16,64,128]{2,1,0:T(8,128)S(1)}, f32[4,16,128]{2,1,0:T(8,128)S(1)}, s32[16,128]{1,0:T(8,128)S(1)}) custom-call(s32[16,128]{1,0:T(8,128)S(1)} %bitcast.7, f32[32,128]{1,0:T(8,128)S(1)} %copy-done.1, f32[16,128]{1,0:T(8,128)S(1)} %get-tuple-element.25.table, f32[2048,128]{1,0:T(8,128)S(1)} %get-tuple-element.26.conc, ...), custom_call_target="tpu_custom_call" | custom-call | tf_op jit(solution)/shard_map/pallas_call | solution.py:425
  10.4 0.0 collective-permute-done.left
  10.4 1.9 %collective-permute-done.1.right = bf16[1040,128]{1,0:T(8,128)(2,1)S(1)} collective-permute-done((bf16[1040,128]{1,0:T(8,128)(2,1)S(1)}, bf16[1040,128]{1,0:T(8,128)(2,1)S(1)}, u32[]{:S(2)}, u32[]{:S(2)}) %collective-permute-start.1) | collective-permute-done | bytes 266272 | tf_op jit(solution)/shard_map/ppermute | solution.py:420
  12.3 1.5 %shard_map.97 = (bf16[16,64,128]{2,1,0:T(8,128)(2,1)S(1)}, bf16[384,128]{1,0:T(8,128)(2,1)S(1)}, bf16[384,128]{1,0:T(8,128)(2,1)S(1)}, bf16[384,128]{1,0:T(8,128)(2,1)S(1)}, f32[16,128]{1,0:T(8,128)S(1)}) custom-call(s32[16,128]{1,0:T(8,128)S(1)} %get-tuple-element.27.bases, bf16[1040,128]{1,0:T(8,128)(2,1)S(1)} %collective-permute-done.left, ...), custom_call_target="tpu_custom_call" | custom-call | tf_op jit(solution)/shard_map/pallas_call | solution.py:441
  13.8 1.6 %collective-permute-done.2.left = bf16[1024,128]{1,0:T(8,128)(2,1)S(1)} collective-permute-done((bf16[1024,128]{1,0:T(8,128)(2,1)S(1)}, bf16[1024,128]{1,0:T(8,128)(2,1)S(1)}, u32[]{:S(2)}, u32[]{:S(2)}) %collective-permute-start.2) | collective-permute-done | bytes 262176 | tf_op jit(solution)/shard_map/ppermute | solution.py:419
  15.4 1.5 %collective-permute-done.3.right = bf16[1024,128]{1,0:T(8,128)(2,1)S(1)} collective-permute-done((bf16[1024,128]{1,0:T(8,128)(2,1)S(1)}, bf16[1024,128]{1,0:T(8,128)(2,1)S(1)}, u32[]{:S(2)}, u32[]{:S(2)}) %collective-permute-start.3) | collective-permute-done | bytes 262176 | tf_op jit(solution)/shard_map/ppermute | solution.py:420
  16.9 0.0 copy-start
  16.9 1.5 %shard_map.100 = (bf16[16,64,128]{2,1,0:T(8,128)(2,1)S(1)}, bf16[384,128]{1,0:T(8,128)(2,1)S(1)}, bf16[384,128]{1,0:T(8,128)(2,1)S(1)}, bf16[384,128]{1,0:T(8,128)(2,1)S(1)}) custom-call(s32[16,128]{1,0:T(8,128)S(1)} %get-tuple-element.27.bases, bf16[1024,128]{1,0:T(8,128)(2,1)S(1)} %collective-permute-done.2.left, ...), custom_call_target="tpu_custom_call" | custom-call | tf_op jit(solution)/shard_map/pallas_call | solution.py:441
  18.4 2.7 %collective-permute-start.10 = (bf16[384,128]{1,0:T(8,128)(2,1)S(1)}, bf16[384,128]{1,0:T(8,128)(2,1)S(1)}, u32[]{:S(2)}, u32[]{:S(2)}) collective-permute-start(bf16[384,128]{1,0:T(8,128)(2,1)S(1)} %get-tuple-element.44), channel_id=1, source_target_pairs={{0,2},{1,3},{2,0},{3,1},{4,6},{5,7},{6,4},{7,5},{8,10},{9,11},{10,... | collective-permute-start | bytes 294920 | tf_op jit(solution)/shard_map/ppermute | solution.py:458
  21.1 1.4 %collective-permute-start.12 = (bf16[384,128]{1,0:T(8,128)(2,1)S(1)}, bf16[384,128]{1,0:T(8,128)(2,1)S(1)}, u32[]{:S(2)}, u32[]{:S(2)}) collective-permute-start(bf16[384,128]{1,0:T(8,128)(2,1)S(1)} %get-tuple-element.46), channel_id=1, source_target_pairs={{0,3},{1,2},{2,1},{3,0},{4,7},{5,6},{6,5},{7,4},{8,11},{9,10},{10,... | collective-permute-start | bytes 294920 | tf_op jit(solution)/shard_map/ppermute | solution.py:458
  22.5 0.2 collective-permute-start.8
  22.7 2.9 %collective-permute-start.11 = (bf16[384,128]{1,0:T(8,128)(2,1)S(1)}, bf16[384,128]{1,0:T(8,128)(2,1)S(1)}, u32[]{:S(2)}, u32[]{:S(2)}) collective-permute-start(bf16[384,128]{1,0:T(8,128)(2,1)S(1)} %get-tuple-element.45), channel_id=1, source_target_pairs={{0,3},{1,2},{2,1},{3,0},{4,7},{5,6},{6,5},{7,4},{8,11},{9,10},{10,... | collective-permute-start | bytes 294920 | tf_op jit(solution)/shard_map/ppermute | solution.py:458
  25.6 0.5 collective-permute-start.7
  26.1 0.4 collective-permute-done.10.refs_3_
  26.5 0.6 %collective-permute-start.9 = (bf16[384,128]{1,0:T(8,128)(2,1)S(1)}, bf16[384,128]{1,0:T(8,128)(2,1)S(1)}, u32[]{:S(2)}, u32[]{:S(2)}) collective-permute-start(bf16[384,128]{1,0:T(8,128)(2,1)S(1)} %get-tuple-element.43), channel_id=1, source_target_pairs={{0,2},{1,3},{2,0},{3,1},{4,6},{5,7},{6,4},{7,5},{8,10},{9,11},{10,... | collective-permute-start | bytes 294920 | tf_op jit(solution)/shard_map/ppermute | solution.py:458
  27.1 0.0 copy-done
  27.1 3.4 %shard_map.101 = (bf16[2048,128]{1,0:T(8,128)(2,1)}, bf16[4,1024,128]{2,1,0:T(8,128)(2,1)}, bf16[256,128]{1,0:T(8,128)(2,1)S(1)}, bf16[256,128]{1,0:T(8,128)(2,1)S(1)}, bf16[256,128]{1,0:T(8,128)(2,1)S(1)}) custom-call(s32[16,128]{1,0:T(8,128)S(1)} %get-tuple-element.27.bases, bf16[128,128]{1,0:T(8,128)(2,1)S(1)} %copy-done, ...), custom_call_target="tpu_custom_call" | custom-call | tf_op jit(solution)/shard_map/pallas_call | solution.py:462
  30.5 0.0 collective-permute-done.12.refs_5_
  30.6 7.0 %collective-permute-start.4 = (bf16[256,128]{1,0:T(8,128)(2,1)S(1)}, bf16[256,128]{1,0:T(8,128)(2,1)S(1)}, u32[]{:S(2)}, u32[]{:S(2)}) collective-permute-start(bf16[256,128]{1,0:T(8,128)(2,1)S(1)} %get-tuple-element.38), channel_id=1, source_target_pairs={{0,1},{1,0},{2,3},{3,2},{4,5},{5,4},{6,7},{7,6},{8,9},{9,8},{10,11... | collective-permute-start | bytes 196616 | tf_op jit(solution)/shard_map/ppermute | solution.py:477
  37.6 0.0 collective-permute-done.8.refs_1_
  37.6 0.0 collective-permute-start.5
  37.6 0.0 collective-permute-done.11.refs_4_
  37.6 2.4 %collective-permute-start.6 = (bf16[256,128]{1,0:T(8,128)(2,1)S(1)}, bf16[256,128]{1,0:T(8,128)(2,1)S(1)}, u32[]{:S(2)}, u32[]{:S(2)}) collective-permute-start(bf16[256,128]{1,0:T(8,128)(2,1)S(1)} %get-tuple-element.40), channel_id=1, source_target_pairs={{0,3},{1,2},{2,1},{3,0},{4,7},{5,6},{6,5},{7,4},{8,11},{9,10},{10,... | collective-permute-start | bytes 196616 | tf_op jit(solution)/shard_map/ppermute | solution.py:477
  40.0 0.0 collective-permute-done.7.refs_0_
  40.1 0.0 collective-permute-done.9.refs_2_
  40.1 2.8 %shard_map.102.refs_3_ = bf16[4,1024,128]{2,1,0:T(8,128)(2,1)} custom-call(bf16[128,128]{1,0:T(8,128)(2,1)S(1)} %copy-done, bf16[384,128]{1,0:T(8,128)(2,1)S(1)} %collective-permute-done.7.refs_0_, bf16[384,128]{1,0:T(8,128)(2,1)S(1)} %collective-permute-done.8.refs_1_, ...), custom_call_target="tpu_custom_call", output_to_operand_aliasing={{}: (7, {})} | custom-call | tf_op jit(solution)/shard_map/pallas_call | solution.py:479
  42.9 0.0 collective-permute-done.4.refs_0_
  42.9 2.2 %collective-permute-done.5.refs_1_ = bf16[256,128]{1,0:T(8,128)(2,1)S(1)} collective-permute-done((bf16[256,128]{1,0:T(8,128)(2,1)S(1)}, bf16[256,128]{1,0:T(8,128)(2,1)S(1)}, u32[]{:S(2)}, u32[]{:S(2)}) %collective-permute-start.5) | collective-permute-done | bytes 65568 | tf_op jit(solution)/shard_map/ppermute | solution.py:477
  45.1 0.0 collective-permute-done.6.refs_2_
  45.1 0.7 %shard_map.103 = bf16[4,1024,128]{2,1,0:T(8,128)(2,1)} custom-call(bf16[256,128]{1,0:T(8,128)(2,1)S(1)} %collective-permute-done.4.refs_0_, bf16[256,128]{1,0:T(8,128)(2,1)S(1)} %collective-permute-done.5.refs_1_, bf16[256,128]{1,0:T(8,128)(2,1)S(1)} %collective-permute-done.6.refs_2_, ...), custom_call_target="tpu_custom_call", output_to_operand_aliasing={{}: (3, {})} | custom-call | tf_op jit(solution)/shard_map/pallas_call | solution.py:491
Async XLA Ops:
  2.0 8.4 %collective-permute-start = (bf16[1040,128]{1,0:T(8,128)(2,1)S(1)}, bf16[1040,128]{1,0:T(8,128)(2,1)S(1)}, u32[]{:S(2)}, u32[]{:S(2)}) collective-permute-start(bf16[1040,128]{1,0:T(8,128)(2,1)S(1)} %get-tuple-element.29.high), channel_id=1, source_target_pairs={{0,4},{4,8},{8,12},{12,16},{16,20},{20,24},{24,28},{28,0},{1,5},{5... | collective-permute-start | bytes 798728 | tf_op jit(solution)/shard_map/ppermute | solution.py:419
  2.6 9.7 %collective-permute-start.1 = (bf16[1040,128]{1,0:T(8,128)(2,1)S(1)}, bf16[1040,128]{1,0:T(8,128)(2,1)S(1)}, u32[]{:S(2)}, u32[]{:S(2)}) collective-permute-start(bf16[1040,128]{1,0:T(8,128)(2,1)S(1)} %get-tuple-element.29.high), channel_id=1, source_target_pairs={{4,0},{8,4},{12,8},{16,12},{20,16},{24,20},{28,24},{0,28},{5,1},{9... | collective-permute-start | bytes 798728 | tf_op jit(solution)/shard_map/ppermute | solution.py:420
  5.5 2.8 %copy-start.1 = (f32[32,128]{1,0:T(8,128)S(1)}, f32[32,128]{1,0:T(8,128)}, u32[]{:S(2)}) copy-start(f32[32,128]{1,0:T(8,128)} %rates.3) | copy-start | bytes 49156
  5.5 2.8 %copy-start.2 = (s32[2048]{0:T(1024)S(1)}, s32[2048]{0:T(1024)}, u32[]{:S(2)}) copy-start(s32[2048]{0:T(1024)} %param.12) | copy-start | bytes 24580
  5.7 9.8 %collective-permute-start.2 = (bf16[1024,128]{1,0:T(8,128)(2,1)S(1)}, bf16[1024,128]{1,0:T(8,128)(2,1)S(1)}, u32[]{:S(2)}, u32[]{:S(2)}) collective-permute-start(bf16[1024,128]{1,0:T(8,128)(2,1)S(1)} %shard_map.98.high), channel_id=1, source_target_pairs={{0,4},{4,8},{8,12},{12,16},{16,20},{20,24},{24,28},{28,0},{1,5},{5... | collective-permute-start | bytes 786440 | tf_op jit(solution)/shard_map/ppermute | solution.py:419
  5.7 11.2 %collective-permute-start.3 = (bf16[1024,128]{1,0:T(8,128)(2,1)S(1)}, bf16[1024,128]{1,0:T(8,128)(2,1)S(1)}, u32[]{:S(2)}, u32[]{:S(2)}) collective-permute-start(bf16[1024,128]{1,0:T(8,128)(2,1)S(1)} %shard_map.98.high), channel_id=1, source_target_pairs={{4,0},{8,4},{12,8},{16,12},{20,16},{24,20},{28,24},{0,28},{5,1},{9... | collective-permute-start | bytes 786440 | tf_op jit(solution)/shard_map/ppermute | solution.py:420
  8.4 1.0 %copy-start.3 = (s32[2048,1]{0,1:T(1,128)S(1)}, s32[2048,1]{0,1:T(1,128)}, u32[]{:S(2)}) copy-start(s32[2048,1]{0,1:T(1,128)} %param.13) | copy-start | bytes 24580
  16.9 10.2 %copy-start = (bf16[128,128]{1,0:T(8,128)(2,1)S(1)}, bf16[128,128]{1,0:T(8,128)(2,1)}, u32[]{:S(2)}) copy-start(bf16[128,128]{1,0:T(8,128)(2,1)} %reaction.3) | copy-start | bytes 98308
  18.4 8.0 %collective-permute-start.10 = (bf16[384,128]{1,0:T(8,128)(2,1)S(1)}, bf16[384,128]{1,0:T(8,128)(2,1)S(1)}, u32[]{:S(2)}, u32[]{:S(2)}) collective-permute-start(bf16[384,128]{1,0:T(8,128)(2,1)S(1)} %get-tuple-element.44), channel_id=1, source_target_pairs={{0,2},{1,3},{2,0},{3,1},{4,6},{5,7},{6,4},{7,5},{8,10},{9,11},{10,... | collective-permute-start | bytes 294920 | tf_op jit(solution)/shard_map/ppermute | solution.py:458
  21.1 9.4 %collective-permute-start.12 = (bf16[384,128]{1,0:T(8,128)(2,1)S(1)}, bf16[384,128]{1,0:T(8,128)(2,1)S(1)}, u32[]{:S(2)}, u32[]{:S(2)}) collective-permute-start(bf16[384,128]{1,0:T(8,128)(2,1)S(1)} %get-tuple-element.46), channel_id=1, source_target_pairs={{0,3},{1,2},{2,1},{3,0},{4,7},{5,6},{6,5},{7,4},{8,11},{9,10},{10,... | collective-permute-start | bytes 294920 | tf_op jit(solution)/shard_map/ppermute | solution.py:458
  22.5 15.1 %collective-permute-start.8 = (bf16[384,128]{1,0:T(8,128)(2,1)S(1)}, bf16[384,128]{1,0:T(8,128)(2,1)S(1)}, u32[]{:S(2)}, u32[]{:S(2)}) collective-permute-start(bf16[384,128]{1,0:T(8,128)(2,1)S(1)} %get-tuple-element.42), channel_id=1, source_target_pairs={{0,1},{1,0},{2,3},{3,2},{4,5},{5,4},{6,7},{7,6},{8,9},{9,8},{10,11... | collective-permute-start | bytes 294920 | tf_op jit(solution)/shard_map/ppermute | solution.py:458
  22.7 14.9 %collective-permute-start.11 = (bf16[384,128]{1,0:T(8,128)(2,1)S(1)}, bf16[384,128]{1,0:T(8,128)(2,1)S(1)}, u32[]{:S(2)}, u32[]{:S(2)}) collective-permute-start(bf16[384,128]{1,0:T(8,128)(2,1)S(1)} %get-tuple-element.45), channel_id=1, source_target_pairs={{0,3},{1,2},{2,1},{3,0},{4,7},{5,6},{6,5},{7,4},{8,11},{9,10},{10,... | collective-permute-start | bytes 294920 | tf_op jit(solution)/shard_map/ppermute | solution.py:458
  25.6 14.4 %collective-permute-start.7 = (bf16[384,128]{1,0:T(8,128)(2,1)S(1)}, bf16[384,128]{1,0:T(8,128)(2,1)S(1)}, u32[]{:S(2)}, u32[]{:S(2)}) collective-permute-start(bf16[384,128]{1,0:T(8,128)(2,1)S(1)} %get-tuple-element.41), channel_id=1, source_target_pairs={{0,1},{1,0},{2,3},{3,2},{4,5},{5,4},{6,7},{7,6},{8,9},{9,8},{10,11... | collective-permute-start | bytes 294920 | tf_op jit(solution)/shard_map/ppermute | solution.py:458
  26.5 13.6 %collective-permute-start.9 = (bf16[384,128]{1,0:T(8,128)(2,1)S(1)}, bf16[384,128]{1,0:T(8,128)(2,1)S(1)}, u32[]{:S(2)}, u32[]{:S(2)}) collective-permute-start(bf16[384,128]{1,0:T(8,128)(2,1)S(1)} %get-tuple-element.43), channel_id=1, source_target_pairs={{0,2},{1,3},{2,0},{3,1},{4,6},{5,7},{6,4},{7,5},{8,10},{9,11},{10,... | collective-permute-start | bytes 294920 | tf_op jit(solution)/shard_map/ppermute | solution.py:458
  30.6 12.4 %collective-permute-start.4 = (bf16[256,128]{1,0:T(8,128)(2,1)S(1)}, bf16[256,128]{1,0:T(8,128)(2,1)S(1)}, u32[]{:S(2)}, u32[]{:S(2)}) collective-permute-start(bf16[256,128]{1,0:T(8,128)(2,1)S(1)} %get-tuple-element.38), channel_id=1, source_target_pairs={{0,1},{1,0},{2,3},{3,2},{4,5},{5,4},{6,7},{7,6},{8,9},{9,8},{10,11... | collective-permute-start | bytes 196616 | tf_op jit(solution)/shard_map/ppermute | solution.py:477
  37.6 7.5 %collective-permute-start.5 = (bf16[256,128]{1,0:T(8,128)(2,1)S(1)}, bf16[256,128]{1,0:T(8,128)(2,1)S(1)}, u32[]{:S(2)}, u32[]{:S(2)}) collective-permute-start(bf16[256,128]{1,0:T(8,128)(2,1)S(1)} %get-tuple-element.39), channel_id=1, source_target_pairs={{0,2},{1,3},{2,0},{3,1},{4,6},{5,7},{6,4},{7,5},{8,10},{9,11},{10,... | collective-permute-start | bytes 196616 | tf_op jit(solution)/shard_map/ppermute | solution.py:477
  37.6 7.5 %collective-permute-start.6 = (bf16[256,128]{1,0:T(8,128)(2,1)S(1)}, bf16[256,128]{1,0:T(8,128)(2,1)S(1)}, u32[]{:S(2)}, u32[]{:S(2)}) collective-permute-start(bf16[256,128]{1,0:T(8,128)(2,1)S(1)} %get-tuple-element.40), channel_id=1, source_target_pairs={{0,3},{1,2},{2,1},{3,0},{4,7},{5,6},{6,5},{7,4},{8,11},{9,10},{10,... | collective-permute-start | bytes 196616 | tf_op jit(solution)/shard_map/ppermute | solution.py:477

commit v3 on v2

--- a/solution.py
+++ b/solution.py
@@ -17,7 +17,7 @@
 CHUNKS = 2
 LOADS = 4
 TILES = 4
-LATE = 4
+LATE = 6
 
 F32 = jnp.float32
 BF16 = jnp.bfloat16
@@ -288,9 +288,9 @@
 def own_kernel(chunks, nblocks, nbal, bases, reaction, keys, *refs):
     starts, out, slots, lates = refs[:chunks], refs[chunks], refs[chunks + 1], refs[chunks + 2 : -6]
     state, done, mine, others, places, sems = refs[-6:]
-    copy = pltpu.make_async_copy(bases, places, sems.at[2])
+    copy = pltpu.make_async_copy(bases, places, sems.at[1])
     copy.start()
-    span, capacity, late = BLK // chunks, slots.shape[1], lates[0].shape[0]
+    span, capacity, late = BLK // chunks, slots.shape[0], lates[0].shape[0]
     for b in range(nblocks):
         for j in range(chunks):
             first = b * BLK + j * span
@@ -322,21 +322,19 @@
             window = placed[k * reach : (k + 1) * reach]
             target[pl.ds(at, edge), :] = target[pl.ds(at, edge), :] + window[:edge]
             target[pl.ds(at + edge, BLK), :] = window[edge:]
-    own = pltpu.make_async_copy(
-        mine.at[pl.ds(0, capacity)], slots.at[lax.axis_index("bal")], sems.at[1]
-    )
-    own.start()
+    slots[...] = mine[:capacity, :]
     for k in range(1, nbal):
         lates[k - 1][...] = others[k - 1, reach : reach + late, :]
     result.wait()
-    own.wait()
-
-
-def slot_kernel(chunks, nbal, reaction, *refs):
+
+
+def slot_kernel(chunks, nbal, reaction, mine, *refs):
     parts = refs[: (nbal - 1) * chunks]
     out, state, result, sems = refs[-4:]
     depth = parts[0].shape[0]
     early = depth * chunks
+    own = pltpu.make_async_copy(mine, out.at[lax.axis_index("bal")], sems.at[nbal - 1])
+    own.start()
     for k in range(1, nbal):
         mine = parts[(k - 1) * chunks : k * chunks]
         for jj in range(chunks):
@@ -359,6 +357,7 @@
             )
         )
         copies[-1].start()
+    own.wait()
     for copy in copies:
         copy.wait()
 
@@ -383,7 +382,7 @@
     chunks = CHUNKS
     span = BLK // chunks
     capacity = 2 * rows // nbal
-    late = capacity // LATE
+    late = capacity * LATE // 16
     depth = (capacity - late) // chunks
 
     shape = jax.ShapeDtypeStruct
@@ -459,18 +458,19 @@
 
     slots = shape((nbal, capacity, LANES), BF16)
     reach = BLK + TILE * chunks
-    conc_out, chem, *lates = call(
+    conc_out, mine, *lates = call(
         functools.partial(own_kernel, chunks, nblocks, nbal),
-        out_shape=[shape((rows, LANES), BF16), slots] + [shape((late, LANES), BF16)] * (nbal - 1),
+        out_shape=[shape((rows, LANES), BF16), shape((capacity, LANES), BF16)]
+            + [shape((late, LANES), BF16)] * (nbal - 1),
         in_specs=[VMEM] * (3 + chunks),
-        out_specs=[ANY, ANY] + [VMEM] * (nbal - 1),
+        out_specs=[ANY] + [VMEM] * nbal,
         scratch_shapes=[
             pltpu.VMEM((rows, LANES), F32),
             pltpu.VMEM((rows, LANES), BF16),
             pltpu.VMEM((capacity + reach, LANES), BF16),
             pltpu.VMEM((nbal - 1, late + 2 * reach, LANES), BF16),
             pltpu.SMEM(bases.shape, jnp.int32),
-            pltpu.SemaphoreType.DMA((3,)),
+            pltpu.SemaphoreType.DMA((2,)),
         ],
     )(bases, reaction, keys, *starts)
     for k in range(1, nbal):
@@ -479,15 +479,14 @@
     chem = call(
         functools.partial(slot_kernel, chunks, nbal),
         out_shape=slots,
-        in_specs=[VMEM] * (1 + chunks * (nbal - 1)) + [ANY],
+        in_specs=[VMEM] * (2 + chunks * (nbal - 1)),
         out_specs=ANY,
         scratch_shapes=[
             pltpu.VMEM(((nbal - 1) * (capacity - late), LANES), F32),
             pltpu.VMEM((nbal - 1, depth // TILE, chunks, TILE, LANES), BF16),
-            pltpu.SemaphoreType.DMA((nbal - 1,)),
+            pltpu.SemaphoreType.DMA((nbal,)),
         ],
-        input_output_aliases={1 + chunks * (nbal - 1): 0},
-    )(reaction, *[part for group in received[1:] for part in group], chem)
+    )(reaction, mine, *[part for group in received[1:] for part in group])
     chem = call(
         functools.partial(late_kernel, nbal),
         out_shape=slots,

time: 46 us -> 48.9 us (1.063)
  waiting for transfers between devices: 7.5 us -> 10.1 us
  starting transfers between devices: 23.9 us -> 25.2 us
  Pallas kernels: 13.6 us -> 12.7 us
    ppermute x6, starting transfers between devices: 8.29 us -> 14.6 us  [step(): lax.ppermute(outs[k], 'bal', [(i, i ^ k) for i in range(nbal)])]
    ppermute x3, starting transfers between devices: 9.49 us -> 4.45 us  [step(): moved = lax.ppermute(lates[k - 1], 'bal', [(i, i ^ k) for i in range(nbal)])]
    ppermute x6, waiting for transfers between devices: 0.4 us -> 5.11 us  [step(): lax.ppermute(outs[k], 'bal', [(i, i ^ k) for i in range(nbal)])]
    ppermute x3, waiting for transfers between devices: 2.18 us -> 0.01 us  [step(): moved = lax.ppermute(lates[k - 1], 'bal', [(i, i ^ k) for i in range(nbal)])]
    pallas_call x1, Pallas kernels: 3.42 us -> 2.82 us  [step(): call(functools.partial(own_kernel, chunks, nblocks, nbal), out_shape=[sha...]
  transfers between devices with their start and end apart: 13 -> 13, of which waited for: 5 -> 5; matrix products, arithmetic and copies ran while one was open for 0% -> 0% of each run, Pallas kernels for 22% -> 19%
where the time goes in v3:
time: 48.9 us; the launch traced here: 48.7 us
  starting transfers between devices  25.2 us (52%)
  Pallas kernels  12.7 us (26%)
  waiting for transfers between devices  10.1 us (21%)
  between operations  0.75 us (2%)
    ppermute x6, starting transfers between devices, step(): lax.ppermute(outs[k], 'bal', [(i, i ^ k) for i in range(nbal)])  14.6 us
    ppermute x2, starting transfers between devices, step(): rights.append(lax.ppermute(outs[0], 'lon', back))  5.57 us
    ppermute x6, waiting for transfers between devices, step(): lax.ppermute(outs[k], 'bal', [(i, i ^ k) for i in range(nbal)])  5.11 us
    ppermute x3, starting transfers between devices, step(): moved = lax.ppermute(lates[k - 1], 'bal', [(i, i ^ k) for i in range(nbal)])  4.45 us
    ppermute x2, waiting for transfers between devices, step(): rights.append(lax.ppermute(outs[0], 'lon', back))  3.34 us
    pallas_call x2, Pallas kernels, step(): call(functools.partial(mix_kernel, chunks, c, nblocks, nbal), out_shape=[...  3.04 us
    pallas_call x1, Pallas kernels, step(): call(functools.partial(own_kernel, chunks, nblocks, nbal), out_shape=[sha...  2.82 us
    pallas_call x1, Pallas kernels, step(): call(functools.partial(slot_kernel, chunks, nbal), out_shape=slots, in_sp...  2.52 us
  transfers between devices with their start and end apart: 13, of which 5 were waited for; matrix products, arithmetic and copies ran while one was open for 0% of the time, Pallas kernels for 19%

profile of v3, /device:TPU:0, one launch (start us, length us, event | category | flops | bytes accessed | tf_op | source)
XLA Modules:
  0.0 48.7 jit_solution(8953579947946913197)
XLA Ops:
  0.6 1.4 %shard_map.95 = (bf16[1040,128]{1,0:T(8,128)(2,1)S(1)}, f32[16,128]{1,0:T(8,128)S(1)}, f32[2048,128]{1,0:T(8,128)S(1)}) custom-call(f32[2048,128]{1,0:T(8,128)} %conc.1, s32[8,16]{1,0:T(8,128)} %bitcast.10, s32[1,16]{1,0:T(1,128)} %bitcast.12, s32[8,16]{1,0:T(8,128)} %bitcast.11), custom_call_target="tpu_custom_call" | custom-call | tf_op jit(solution)/shard_map/pallas_call | solution.py:406
  2.0 0.5 %collective-permute-start = (bf16[1040,128]{1,0:T(8,128)(2,1)S(1)}, bf16[1040,128]{1,0:T(8,128)(2,1)S(1)}, u32[]{:S(2)}, u32[]{:S(2)}) collective-permute-start(bf16[1040,128]{1,0:T(8,128)(2,1)S(1)} %get-tuple-element.29.high), channel_id=1, source_target_pairs={{0,4},{4,8},{8,12},{12,16},{16,20},{20,24},{24,28},{28,0},{1,5},{5... | collective-permute-start | bytes 798728 | tf_op jit(solution)/shard_map/ppermute | solution.py:418
  2.6 2.9 %collective-permute-start.1 = (bf16[1040,128]{1,0:T(8,128)(2,1)S(1)}, bf16[1040,128]{1,0:T(8,128)(2,1)S(1)}, u32[]{:S(2)}, u32[]{:S(2)}) collective-permute-start(bf16[1040,128]{1,0:T(8,128)(2,1)S(1)} %get-tuple-element.29.high), channel_id=1, source_target_pairs={{4,0},{8,4},{12,8},{16,12},{20,16},{24,20},{28,24},{0,28},{5,1},{9... | collective-permute-start | bytes 798728 | tf_op jit(solution)/shard_map/ppermute | solution.py:419
  5.5 0.0 copy-start.1
  5.5 0.0 copy-start.2
  5.5 0.1 shard_map.98.high
  5.7 0.1 collective-permute-start.2
  5.7 2.6 %collective-permute-start.3 = (bf16[1024,128]{1,0:T(8,128)(2,1)S(1)}, bf16[1024,128]{1,0:T(8,128)(2,1)S(1)}, u32[]{:S(2)}, u32[]{:S(2)}) collective-permute-start(bf16[1024,128]{1,0:T(8,128)(2,1)S(1)} %shard_map.98.high), channel_id=1, source_target_pairs={{4,0},{8,4},{12,8},{16,12},{20,16},{24,20},{28,24},{0,28},{5,1},{9... | collective-permute-start | bytes 786440 | tf_op jit(solution)/shard_map/ppermute | solution.py:419
  8.4 0.0 copy-done.1
  8.4 0.0 copy-done.2
  8.4 0.0 copy-start.3
  8.4 1.0 %shard_map.99 = (f32[16,64,128]{2,1,0:T(8,128)S(1)}, f32[16,64,128]{2,1,0:T(8,128)S(1)}) custom-call(s32[16,128]{1,0:T(8,128)S(1)} %bitcast.6, f32[32,128]{1,0:T(8,128)S(1)} %copy-done.1, f32[16,128]{1,0:T(8,128)S(1)} %get-tuple-element.25.table, f32[2048,128]{1,0:T(8,128)S(1)} %get-tuple-element.26.conc), custom_call_target="tpu_custom_call" | custom-call | tf_op jit(solution)/shard_map/pallas_call | solution.py:424
  9.4 0.0 copy-done.3
  9.4 1.0 %shard_map.96 = (f32[16,64,128]{2,1,0:T(8,128)S(1)}, f32[16,64,128]{2,1,0:T(8,128)S(1)}, f32[4,16,128]{2,1,0:T(8,128)S(1)}, s32[16,128]{1,0:T(8,128)S(1)}) custom-call(s32[16,128]{1,0:T(8,128)S(1)} %bitcast.7, f32[32,128]{1,0:T(8,128)S(1)} %copy-done.1, f32[16,128]{1,0:T(8,128)S(1)} %get-tuple-element.25.table, f32[2048,128]{1,0:T(8,128)S(1)} %get-tuple-element.26.conc, ...), custom_call_target="tpu_custom_call" | custom-call | tf_op jit(solution)/shard_map/pallas_call | solution.py:424
  10.4 0.0 collective-permute-done.left
  10.4 1.9 %collective-permute-done.1.right = bf16[1040,128]{1,0:T(8,128)(2,1)S(1)} collective-permute-done((bf16[1040,128]{1,0:T(8,128)(2,1)S(1)}, bf16[1040,128]{1,0:T(8,128)(2,1)S(1)}, u32[]{:S(2)}, u32[]{:S(2)}) %collective-permute-start.1) | collective-permute-done | bytes 266272 | tf_op jit(solution)/shard_map/ppermute | solution.py:419
  12.3 1.5 %shard_map.97 = (bf16[16,64,128]{2,1,0:T(8,128)(2,1)S(1)}, bf16[320,128]{1,0:T(8,128)(2,1)S(1)}, bf16[320,128]{1,0:T(8,128)(2,1)S(1)}, bf16[320,128]{1,0:T(8,128)(2,1)S(1)}, f32[16,128]{1,0:T(8,128)S(1)}) custom-call(s32[16,128]{1,0:T(8,128)S(1)} %get-tuple-element.27.bases, bf16[1040,128]{1,0:T(8,128)(2,1)S(1)} %collective-permute-done.left, ...), custom_call_target="tpu_custom_call" | custom-call | tf_op jit(solution)/shard_map/pallas_call | solution.py:440
  13.8 1.6 %collective-permute-done.2.left = bf16[1024,128]{1,0:T(8,128)(2,1)S(1)} collective-permute-done((bf16[1024,128]{1,0:T(8,128)(2,1)S(1)}, bf16[1024,128]{1,0:T(8,128)(2,1)S(1)}, u32[]{:S(2)}, u32[]{:S(2)}) %collective-permute-start.2) | collective-permute-done | bytes 262176 | tf_op jit(solution)/shard_map/ppermute | solution.py:418
  15.4 1.5 %collective-permute-done.3.right = bf16[1024,128]{1,0:T(8,128)(2,1)S(1)} collective-permute-done((bf16[1024,128]{1,0:T(8,128)(2,1)S(1)}, bf16[1024,128]{1,0:T(8,128)(2,1)S(1)}, u32[]{:S(2)}, u32[]{:S(2)}) %collective-permute-start.3) | collective-permute-done | bytes 262176 | tf_op jit(solution)/shard_map/ppermute | solution.py:419
  16.9 0.0 copy-start
  16.9 1.5 %shard_map.100 = (bf16[16,64,128]{2,1,0:T(8,128)(2,1)S(1)}, bf16[320,128]{1,0:T(8,128)(2,1)S(1)}, bf16[320,128]{1,0:T(8,128)(2,1)S(1)}, bf16[320,128]{1,0:T(8,128)(2,1)S(1)}) custom-call(s32[16,128]{1,0:T(8,128)S(1)} %get-tuple-element.27.bases, bf16[1024,128]{1,0:T(8,128)(2,1)S(1)} %collective-permute-done.2.left, ...), custom_call_target="tpu_custom_call" | custom-call | tf_op jit(solution)/shard_map/pallas_call | solution.py:440
  18.4 2.7 %collective-permute-start.10 = (bf16[320,128]{1,0:T(8,128)(2,1)S(1)}, bf16[320,128]{1,0:T(8,128)(2,1)S(1)}, u32[]{:S(2)}, u32[]{:S(2)}) collective-permute-start(bf16[320,128]{1,0:T(8,128)(2,1)S(1)} %get-tuple-element.45), channel_id=1, source_target_pairs={{0,2},{1,3},{2,0},{3,1},{4,6},{5,7},{6,4},{7,5},{8,10},{9,11},{10,... | collective-permute-start | bytes 245768 | tf_op jit(solution)/shard_map/ppermute | solution.py:457
  21.1 1.3 %collective-permute-start.12 = (bf16[320,128]{1,0:T(8,128)(2,1)S(1)}, bf16[320,128]{1,0:T(8,128)(2,1)S(1)}, u32[]{:S(2)}, u32[]{:S(2)}) collective-permute-start(bf16[320,128]{1,0:T(8,128)(2,1)S(1)} %get-tuple-element.47), channel_id=1, source_target_pairs={{0,3},{1,2},{2,1},{3,0},{4,7},{5,6},{6,5},{7,4},{8,11},{9,10},{10,... | collective-permute-start | bytes 245768 | tf_op jit(solution)/shard_map/ppermute | solution.py:457
  22.5 0.3 collective-permute-start.8
  22.7 2.9 %collective-permute-start.11 = (bf16[320,128]{1,0:T(8,128)(2,1)S(1)}, bf16[320,128]{1,0:T(8,128)(2,1)S(1)}, u32[]{:S(2)}, u32[]{:S(2)}) collective-permute-start(bf16[320,128]{1,0:T(8,128)(2,1)S(1)} %get-tuple-element.46), channel_id=1, source_target_pairs={{0,3},{1,2},{2,1},{3,0},{4,7},{5,6},{6,5},{7,4},{8,11},{9,10},{10,... | collective-permute-start | bytes 245768 | tf_op jit(solution)/shard_map/ppermute | solution.py:457
  25.7 0.0 copy-done
  25.7 2.8 %shard_map.101 = (bf16[2048,128]{1,0:T(8,128)(2,1)}, bf16[1024,128]{1,0:T(8,128)(2,1)S(1)}, bf16[384,128]{1,0:T(8,128)(2,1)S(1)}, bf16[384,128]{1,0:T(8,128)(2,1)S(1)}, bf16[384,128]{1,0:T(8,128)(2,1)S(1)}) custom-call(s32[16,128]{1,0:T(8,128)S(1)} %get-tuple-element.27.bases, bf16[128,128]{1,0:T(8,128)(2,1)S(1)} %copy-done, ...), custom_call_target="tpu_custom_call" | custom-call | tf_op jit(solution)/shard_map/pallas_call | solution.py:461
  28.5 0.5 collective-permute-start.4
  29.0 0.0 collective-permute-done.10.refs_3_
  29.0 1.0 %collective-permute-start.5 = (bf16[384,128]{1,0:T(8,128)(2,1)S(1)}, bf16[384,128]{1,0:T(8,128)(2,1)S(1)}, u32[]{:S(2)}, u32[]{:S(2)}) collective-permute-start(bf16[384,128]{1,0:T(8,128)(2,1)S(1)} %get-tuple-element.39), channel_id=1, source_target_pairs={{0,2},{1,3},{2,0},{3,1},{4,6},{5,7},{6,4},{7,5},{8,10},{9,11},{10,... | collective-permute-start | bytes 294920 | tf_op jit(solution)/shard_map/ppermute | solution.py:477
  30.0 0.0 collective-permute-done.12.refs_5_
  30.0 2.9 %collective-permute-start.6 = (bf16[384,128]{1,0:T(8,128)(2,1)S(1)}, bf16[384,128]{1,0:T(8,128)(2,1)S(1)}, u32[]{:S(2)}, u32[]{:S(2)}) collective-permute-start(bf16[384,128]{1,0:T(8,128)(2,1)S(1)} %get-tuple-element.40), channel_id=1, source_target_pairs={{0,3},{1,2},{2,1},{3,0},{4,7},{5,6},{6,5},{7,4},{8,11},{9,10},{10,... | collective-permute-start | bytes 294920 | tf_op jit(solution)/shard_map/ppermute | solution.py:477
  33.0 0.0 collective-permute-done.8.refs_1_
  33.0 2.0 %collective-permute-start.7 = (bf16[320,128]{1,0:T(8,128)(2,1)S(1)}, bf16[320,128]{1,0:T(8,128)(2,1)S(1)}, u32[]{:S(2)}, u32[]{:S(2)}) collective-permute-start(bf16[320,128]{1,0:T(8,128)(2,1)S(1)} %get-tuple-element.42), channel_id=1, source_target_pairs={{0,1},{1,0},{2,3},{3,2},{4,5},{5,4},{6,7},{7,6},{8,9},{9,8},{10,11... | collective-permute-start | bytes 245768 | tf_op jit(solution)/shard_map/ppermute | solution.py:457
  34.9 0.0 collective-permute-done.11.refs_4_
  34.9 5.4 %collective-permute-start.9 = (bf16[320,128]{1,0:T(8,128)(2,1)S(1)}, bf16[320,128]{1,0:T(8,128)(2,1)S(1)}, u32[]{:S(2)}, u32[]{:S(2)}) collective-permute-start(bf16[320,128]{1,0:T(8,128)(2,1)S(1)} %get-tuple-element.44), channel_id=1, source_target_pairs={{0,2},{1,3},{2,0},{3,1},{4,6},{5,7},{6,4},{7,5},{8,10},{9,11},{10,... | collective-permute-start | bytes 245768 | tf_op jit(solution)/shard_map/ppermute | solution.py:457
  40.3 0.8 %collective-permute-done.7.refs_0_ = bf16[320,128]{1,0:T(8,128)(2,1)S(1)} collective-permute-done((bf16[320,128]{1,0:T(8,128)(2,1)S(1)}, bf16[320,128]{1,0:T(8,128)(2,1)S(1)}, u32[]{:S(2)}, u32[]{:S(2)}) %collective-permute-start.7) | collective-permute-done | bytes 81952 | tf_op jit(solution)/shard_map/ppermute | solution.py:457
  41.1 4.3 %collective-permute-done.9.refs_2_ = bf16[320,128]{1,0:T(8,128)(2,1)S(1)} collective-permute-done((bf16[320,128]{1,0:T(8,128)(2,1)S(1)}, bf16[320,128]{1,0:T(8,128)(2,1)S(1)}, u32[]{:S(2)}, u32[]{:S(2)}) %collective-permute-start.9) | collective-permute-done | bytes 81952 | tf_op jit(solution)/shard_map/ppermute | solution.py:457
  45.4 2.5 %shard_map.102.refs_3_ = bf16[4,1024,128]{2,1,0:T(8,128)(2,1)} custom-call(bf16[128,128]{1,0:T(8,128)(2,1)S(1)} %copy-done, bf16[1024,128]{1,0:T(8,128)(2,1)S(1)} %get-tuple-element.41.mine, bf16[320,128]{1,0:T(8,128)(2,1)S(1)} %collective-permute-done.7.refs_0_, bf16[320,128]{1,0:T(8,128)(2,1)S(1)} %collective-permute-done.8.refs_1_, ...), custom_call_target="tpu_custom_call" | custom-call | tf_op jit(solution)/shard_map/pallas_call | solution.py:479
  48.0 0.0 collective-permute-done.4.refs_0_
  48.0 0.0 collective-permute-done.5.refs_1_
  48.0 0.0 collective-permute-done.6.refs_2_
  48.0 0.7 %shard_map.103 = bf16[4,1024,128]{2,1,0:T(8,128)(2,1)} custom-call(bf16[384,128]{1,0:T(8,128)(2,1)S(1)} %collective-permute-done.4.refs_0_, bf16[384,128]{1,0:T(8,128)(2,1)S(1)} %collective-permute-done.5.refs_1_, bf16[384,128]{1,0:T(8,128)(2,1)S(1)} %collective-permute-done.6.refs_2_, ...), custom_call_target="tpu_custom_call", output_to_operand_aliasing={{}: (3, {})} | custom-call | tf_op jit(solution)/shard_map/pallas_call | solution.py:490
Async XLA Ops:
  2.0 8.4 %collective-permute-start = (bf16[1040,128]{1,0:T(8,128)(2,1)S(1)}, bf16[1040,128]{1,0:T(8,128)(2,1)S(1)}, u32[]{:S(2)}, u32[]{:S(2)}) collective-permute-start(bf16[1040,128]{1,0:T(8,128)(2,1)S(1)} %get-tuple-element.29.high), channel_id=1, source_target_pairs={{0,4},{4,8},{8,12},{12,16},{16,20},{20,24},{24,28},{28,0},{1,5},{5... | collective-permute-start | bytes 798728 | tf_op jit(solution)/shard_map/ppermute | solution.py:418
  2.6 9.7 %collective-permute-start.1 = (bf16[1040,128]{1,0:T(8,128)(2,1)S(1)}, bf16[1040,128]{1,0:T(8,128)(2,1)S(1)}, u32[]{:S(2)}, u32[]{:S(2)}) collective-permute-start(bf16[1040,128]{1,0:T(8,128)(2,1)S(1)} %get-tuple-element.29.high), channel_id=1, source_target_pairs={{4,0},{8,4},{12,8},{16,12},{20,16},{24,20},{28,24},{0,28},{5,1},{9... | collective-permute-start | bytes 798728 | tf_op jit(solution)/shard_map/ppermute | solution.py:419
  5.5 2.8 %copy-start.1 = (f32[32,128]{1,0:T(8,128)S(1)}, f32[32,128]{1,0:T(8,128)}, u32[]{:S(2)}) copy-start(f32[32,128]{1,0:T(8,128)} %rates.3) | copy-start | bytes 49156
  5.5 2.8 %copy-start.2 = (s32[2048]{0:T(1024)S(1)}, s32[2048]{0:T(1024)}, u32[]{:S(2)}) copy-start(s32[2048]{0:T(1024)} %param.12) | copy-start | bytes 24580
  5.7 9.8 %collective-permute-start.2 = (bf16[1024,128]{1,0:T(8,128)(2,1)S(1)}, bf16[1024,128]{1,0:T(8,128)(2,1)S(1)}, u32[]{:S(2)}, u32[]{:S(2)}) collective-permute-start(bf16[1024,128]{1,0:T(8,128)(2,1)S(1)} %shard_map.98.high), channel_id=1, source_target_pairs={{0,4},{4,8},{8,12},{12,16},{16,20},{20,24},{24,28},{28,0},{1,5},{5... | collective-permute-start | bytes 786440 | tf_op jit(solution)/shard_map/ppermute | solution.py:418
  5.7 11.2 %collective-permute-start.3 = (bf16[1024,128]{1,0:T(8,128)(2,1)S(1)}, bf16[1024,128]{1,0:T(8,128)(2,1)S(1)}, u32[]{:S(2)}, u32[]{:S(2)}) collective-permute-start(bf16[1024,128]{1,0:T(8,128)(2,1)S(1)} %shard_map.98.high), channel_id=1, source_target_pairs={{4,0},{8,4},{12,8},{16,12},{20,16},{24,20},{28,24},{0,28},{5,1},{9... | collective-permute-start | bytes 786440 | tf_op jit(solution)/shard_map/ppermute | solution.py:419
  8.4 1.0 %copy-start.3 = (s32[2048,1]{0,1:T(1,128)S(1)}, s32[2048,1]{0,1:T(1,128)}, u32[]{:S(2)}) copy-start(s32[2048,1]{0,1:T(1,128)} %param.13) | copy-start | bytes 24580
  16.9 8.8 %copy-start = (bf16[128,128]{1,0:T(8,128)(2,1)S(1)}, bf16[128,128]{1,0:T(8,128)(2,1)}, u32[]{:S(2)}) copy-start(bf16[128,128]{1,0:T(8,128)(2,1)} %reaction.3) | copy-start | bytes 98308
  18.4 10.6 %collective-permute-start.10 = (bf16[320,128]{1,0:T(8,128)(2,1)S(1)}, bf16[320,128]{1,0:T(8,128)(2,1)S(1)}, u32[]{:S(2)}, u32[]{:S(2)}) collective-permute-start(bf16[320,128]{1,0:T(8,128)(2,1)S(1)} %get-tuple-element.45), channel_id=1, source_target_pairs={{0,2},{1,3},{2,0},{3,1},{4,6},{5,7},{6,4},{7,5},{8,10},{9,11},{10,... | collective-permute-start | bytes 245768 | tf_op jit(solution)/shard_map/ppermute | solution.py:457
  21.1 8.9 %collective-permute-start.12 = (bf16[320,128]{1,0:T(8,128)(2,1)S(1)}, bf16[320,128]{1,0:T(8,128)(2,1)S(1)}, u32[]{:S(2)}, u32[]{:S(2)}) collective-permute-start(bf16[320,128]{1,0:T(8,128)(2,1)S(1)} %get-tuple-element.47), channel_id=1, source_target_pairs={{0,3},{1,2},{2,1},{3,0},{4,7},{5,6},{6,5},{7,4},{8,11},{9,10},{10,... | collective-permute-start | bytes 245768 | tf_op jit(solution)/shard_map/ppermute | solution.py:457
  22.5 10.5 %collective-permute-start.8 = (bf16[320,128]{1,0:T(8,128)(2,1)S(1)}, bf16[320,128]{1,0:T(8,128)(2,1)S(1)}, u32[]{:S(2)}, u32[]{:S(2)}) collective-permute-start(bf16[320,128]{1,0:T(8,128)(2,1)S(1)} %get-tuple-element.43), channel_id=1, source_target_pairs={{0,1},{1,0},{2,3},{3,2},{4,5},{5,4},{6,7},{7,6},{8,9},{9,8},{10,11... | collective-permute-start | bytes 245768 | tf_op jit(solution)/shard_map/ppermute | solution.py:457
  22.7 12.2 %collective-permute-start.11 = (bf16[320,128]{1,0:T(8,128)(2,1)S(1)}, bf16[320,128]{1,0:T(8,128)(2,1)S(1)}, u32[]{:S(2)}, u32[]{:S(2)}) collective-permute-start(bf16[320,128]{1,0:T(8,128)(2,1)S(1)} %get-tuple-element.46), channel_id=1, source_target_pairs={{0,3},{1,2},{2,1},{3,0},{4,7},{5,6},{6,5},{7,4},{8,11},{9,10},{10,... | collective-permute-start | bytes 245768 | tf_op jit(solution)/shard_map/ppermute | solution.py:457
  28.5 19.5 %collective-permute-start.4 = (bf16[384,128]{1,0:T(8,128)(2,1)S(1)}, bf16[384,128]{1,0:T(8,128)(2,1)S(1)}, u32[]{:S(2)}, u32[]{:S(2)}) collective-permute-start(bf16[384,128]{1,0:T(8,128)(2,1)S(1)} %get-tuple-element.38), channel_id=1, source_target_pairs={{0,1},{1,0},{2,3},{3,2},{4,5},{5,4},{6,7},{7,6},{8,9},{9,8},{10,11... | collective-permute-start | bytes 294920 | tf_op jit(solution)/shard_map/ppermute | solution.py:477
  29.0 19.0 %collective-permute-start.5 = (bf16[384,128]{1,0:T(8,128)(2,1)S(1)}, bf16[384,128]{1,0:T(8,128)(2,1)S(1)}, u32[]{:S(2)}, u32[]{:S(2)}) collective-permute-start(bf16[384,128]{1,0:T(8,128)(2,1)S(1)} %get-tuple-element.39), channel_id=1, source_target_pairs={{0,2},{1,3},{2,0},{3,1},{4,6},{5,7},{6,4},{7,5},{8,10},{9,11},{10,... | collective-permute-start | bytes 294920 | tf_op jit(solution)/shard_map/ppermute | solution.py:477
  30.0 17.9 %collective-permute-start.6 = (bf16[384,128]{1,0:T(8,128)(2,1)S(1)}, bf16[384,128]{1,0:T(8,128)(2,1)S(1)}, u32[]{:S(2)}, u32[]{:S(2)}) collective-permute-start(bf16[384,128]{1,0:T(8,128)(2,1)S(1)} %get-tuple-element.40), channel_id=1, source_target_pairs={{0,3},{1,2},{2,1},{3,0},{4,7},{5,6},{6,5},{7,4},{8,11},{9,10},{10,... | collective-permute-start | bytes 294920 | tf_op jit(solution)/shard_map/ppermute | solution.py:477
  33.0 8.1 %collective-permute-start.7 = (bf16[320,128]{1,0:T(8,128)(2,1)S(1)}, bf16[320,128]{1,0:T(8,128)(2,1)S(1)}, u32[]{:S(2)}, u32[]{:S(2)}) collective-permute-start(bf16[320,128]{1,0:T(8,128)(2,1)S(1)} %get-tuple-element.42), channel_id=1, source_target_pairs={{0,1},{1,0},{2,3},{3,2},{4,5},{5,4},{6,7},{7,6},{8,9},{9,8},{10,11... | collective-permute-start | bytes 245768 | tf_op jit(solution)/shard_map/ppermute | solution.py:457
  34.9 10.5 %collective-permute-start.9 = (bf16[320,128]{1,0:T(8,128)(2,1)S(1)}, bf16[320,128]{1,0:T(8,128)(2,1)S(1)}, u32[]{:S(2)}, u32[]{:S(2)}) collective-permute-start(bf16[320,128]{1,0:T(8,128)(2,1)S(1)} %get-tuple-element.44), channel_id=1, source_target_pairs={{0,2},{1,3},{2,0},{3,1},{4,6},{5,7},{6,4},{7,5},{8,10},{9,11},{10,... | collective-permute-start | bytes 245768 | tf_op jit(solution)/shard_map/ppermute | solution.py:457

commit v4 on v3

--- a/solution.py
+++ b/solution.py
@@ -122,14 +122,16 @@
 
 
 def couple(table, first, blocks, nblocks):
-    columns = blocks * TILE
-    pick = (iota((LANES, columns), 1) >> SHIFT) + first == iota((LANES, columns), 0)
-    wide = dot(table.astype(BF16), jnp.where(pick, 1.0, 0.0).astype(BF16))
     same = iota((TILE, LANES), 0) == (iota((TILE, LANES), 1) & (TILE - 1))
     same = jnp.where(same, 1.0, 0.0)
+    group = iota((nblocks, LANES), 1) >> SHIFT
     parts = []
-    for c in range(0, columns, LANES):
-        part = jnp.broadcast_to(wide[:, None, c : c + LANES], (nblocks, TILE, LANES)) * same[None]
+    for h in range(first, first + blocks, LANES // TILE):
+        wide = None
+        for j in range(LANES // TILE):
+            column = jnp.broadcast_to(table[:, h + j : h + j + 1], (nblocks, LANES))
+            wide = column if wide is None else jnp.where(group == j, column, wide)
+        part = jnp.broadcast_to(wide[:, None, :], (nblocks, TILE, LANES)) * same[None]
         parts.append(part.reshape(nblocks * TILE, LANES).astype(BF16))
     return jnp.concatenate(parts, axis=1)
 
@@ -296,14 +298,14 @@
             first = b * BLK + j * span
             rows = regroup([starts[c][b] for c in range(chunks)], j, chunks)
             state[first : first + span, :] = rows.astype(F32) * 4.0
+    mine[...] = jnp.zeros(mine.shape, BF16)
+    others[...] = jnp.zeros(others.shape, BF16)
     chemistry(state, reaction)
     done[...] = (state[...] * 0.25).astype(BF16)
     result = pltpu.make_async_copy(done, out, sems.at[0])
     result.start()
     edge = TILE * chunks
     reach = BLK + edge
-    mine[...] = jnp.zeros(mine.shape, BF16)
-    others[...] = jnp.zeros(others.shape, BF16)
     mark = iota((reach, LANES), 0).astype(F32)
     copy.wait()
     for b in range(nblocks):

time: 48.9 us -> 48.8 us (level)
  no operation moved by 1% of the time
where the time goes in v4:
time: 48.8 us; the launch traced here: 48.7 us
  starting transfers between devices  25.2 us (52%)
  Pallas kernels  12.7 us (26%)
  waiting for transfers between devices  10 us (20%)
  between operations  0.75 us (2%)
    ppermute x6, starting transfers between devices, step(): lax.ppermute(outs[k], 'bal', [(i, i ^ k) for i in range(nbal)])  14.6 us
    ppermute x2, starting transfers between devices, step(): rights.append(lax.ppermute(outs[0], 'lon', back))  5.57 us
    ppermute x6, waiting for transfers between devices, step(): lax.ppermute(outs[k], 'bal', [(i, i ^ k) for i in range(nbal)])  5.12 us
    ppermute x3, starting transfers between devices, step(): moved = lax.ppermute(lates[k - 1], 'bal', [(i, i ^ k) for i in range(nbal)])  4.45 us
    ppermute x2, waiting for transfers between devices, step(): rights.append(lax.ppermute(outs[0], 'lon', back))  3.22 us
    pallas_call x2, Pallas kernels, step(): call(functools.partial(mix_kernel, chunks, c, nblocks, nbal), out_shape=[...  2.89 us
    pallas_call x1, Pallas kernels, step(): call(functools.partial(own_kernel, chunks, nblocks, nbal), out_shape=[sha...  2.82 us
    pallas_call x1, Pallas kernels, step(): call(functools.partial(slot_kernel, chunks, nbal), out_shape=slots, in_sp...  2.52 us
  transfers between devices with their start and end apart: 13, of which 5 were waited for; matrix products, arithmetic and copies ran while one was open for 0% of the time, Pallas kernels for 19%

profile of v4, /device:TPU:0, one launch (start us, length us, event | category | flops | bytes accessed | tf_op | source)
XLA Modules:
  0.0 48.7 jit_solution(11739995490648144160)
XLA Ops:
  0.6 1.4 %shard_map.95 = (bf16[1040,128]{1,0:T(8,128)(2,1)S(1)}, f32[16,128]{1,0:T(8,128)S(1)}, f32[2048,128]{1,0:T(8,128)S(1)}) custom-call(f32[2048,128]{1,0:T(8,128)} %conc.1, s32[8,16]{1,0:T(8,128)} %bitcast.10, s32[1,16]{1,0:T(1,128)} %bitcast.12, s32[8,16]{1,0:T(8,128)} %bitcast.11), custom_call_target="tpu_custom_call" | custom-call | tf_op jit(solution)/shard_map/pallas_call | solution.py:408
  2.0 0.5 %collective-permute-start = (bf16[1040,128]{1,0:T(8,128)(2,1)S(1)}, bf16[1040,128]{1,0:T(8,128)(2,1)S(1)}, u32[]{:S(2)}, u32[]{:S(2)}) collective-permute-start(bf16[1040,128]{1,0:T(8,128)(2,1)S(1)} %get-tuple-element.29.high), channel_id=1, source_target_pairs={{0,4},{4,8},{8,12},{12,16},{16,20},{20,24},{24,28},{28,0},{1,5},{5... | collective-permute-start | bytes 798728 | tf_op jit(solution)/shard_map/ppermute | solution.py:420
  2.6 2.9 %collective-permute-start.1 = (bf16[1040,128]{1,0:T(8,128)(2,1)S(1)}, bf16[1040,128]{1,0:T(8,128)(2,1)S(1)}, u32[]{:S(2)}, u32[]{:S(2)}) collective-permute-start(bf16[1040,128]{1,0:T(8,128)(2,1)S(1)} %get-tuple-element.29.high), channel_id=1, source_target_pairs={{4,0},{8,4},{12,8},{16,12},{20,16},{24,20},{28,24},{0,28},{5,1},{9... | collective-permute-start | bytes 798728 | tf_op jit(solution)/shard_map/ppermute | solution.py:421
  5.5 0.0 copy-start.1
  5.5 0.0 copy-start.2
  5.5 0.1 shard_map.98.high
  5.7 0.1 collective-permute-start.2
  5.7 2.6 %collective-permute-start.3 = (bf16[1024,128]{1,0:T(8,128)(2,1)S(1)}, bf16[1024,128]{1,0:T(8,128)(2,1)S(1)}, u32[]{:S(2)}, u32[]{:S(2)}) collective-permute-start(bf16[1024,128]{1,0:T(8,128)(2,1)S(1)} %shard_map.98.high), channel_id=1, source_target_pairs={{4,0},{8,4},{12,8},{16,12},{20,16},{24,20},{28,24},{0,28},{5,1},{9... | collective-permute-start | bytes 786440 | tf_op jit(solution)/shard_map/ppermute | solution.py:421
  8.4 0.0 copy-done.1
  8.4 0.0 copy-done.2
  8.4 0.0 copy-start.3
  8.4 1.1 %shard_map.99 = (f32[16,64,128]{2,1,0:T(8,128)S(1)}, f32[16,64,128]{2,1,0:T(8,128)S(1)}) custom-call(s32[16,128]{1,0:T(8,128)S(1)} %bitcast.6, f32[32,128]{1,0:T(8,128)S(1)} %copy-done.1, f32[16,128]{1,0:T(8,128)S(1)} %get-tuple-element.25.table, f32[2048,128]{1,0:T(8,128)S(1)} %get-tuple-element.26.conc), custom_call_target="tpu_custom_call" | custom-call | tf_op jit(solution)/shard_map/pallas_call | solution.py:426
  9.5 0.0 copy-done.3
  9.5 1.1 %shard_map.96 = (f32[16,64,128]{2,1,0:T(8,128)S(1)}, f32[16,64,128]{2,1,0:T(8,128)S(1)}, f32[4,16,128]{2,1,0:T(8,128)S(1)}, s32[16,128]{1,0:T(8,128)S(1)}) custom-call(s32[16,128]{1,0:T(8,128)S(1)} %bitcast.7, f32[32,128]{1,0:T(8,128)S(1)} %copy-done.1, f32[16,128]{1,0:T(8,128)S(1)} %get-tuple-element.25.table, f32[2048,128]{1,0:T(8,128)S(1)} %get-tuple-element.26.conc, ...), custom_call_target="tpu_custom_call" | custom-call | tf_op jit(solution)/shard_map/pallas_call | solution.py:426
  10.5 0.0 collective-permute-done.left
  10.6 1.8 %collective-permute-done.1.right = bf16[1040,128]{1,0:T(8,128)(2,1)S(1)} collective-permute-done((bf16[1040,128]{1,0:T(8,128)(2,1)S(1)}, bf16[1040,128]{1,0:T(8,128)(2,1)S(1)}, u32[]{:S(2)}, u32[]{:S(2)}) %collective-permute-start.1) | collective-permute-done | bytes 266272 | tf_op jit(solution)/shard_map/ppermute | solution.py:421
  12.3 1.4 %shard_map.97 = (bf16[16,64,128]{2,1,0:T(8,128)(2,1)S(1)}, bf16[320,128]{1,0:T(8,128)(2,1)S(1)}, bf16[320,128]{1,0:T(8,128)(2,1)S(1)}, bf16[320,128]{1,0:T(8,128)(2,1)S(1)}, f32[16,128]{1,0:T(8,128)S(1)}) custom-call(s32[16,128]{1,0:T(8,128)S(1)} %get-tuple-element.27.bases, bf16[1040,128]{1,0:T(8,128)(2,1)S(1)} %collective-permute-done.left, ...), custom_call_target="tpu_custom_call" | custom-call | tf_op jit(solution)/shard_map/pallas_call | solution.py:442
  13.8 1.7 %collective-permute-done.2.left = bf16[1024,128]{1,0:T(8,128)(2,1)S(1)} collective-permute-done((bf16[1024,128]{1,0:T(8,128)(2,1)S(1)}, bf16[1024,128]{1,0:T(8,128)(2,1)S(1)}, u32[]{:S(2)}, u32[]{:S(2)}) %collective-permute-start.2) | collective-permute-done | bytes 262176 | tf_op jit(solution)/shard_map/ppermute | solution.py:420
  15.4 1.5 %collective-permute-done.3.right = bf16[1024,128]{1,0:T(8,128)(2,1)S(1)} collective-permute-done((bf16[1024,128]{1,0:T(8,128)(2,1)S(1)}, bf16[1024,128]{1,0:T(8,128)(2,1)S(1)}, u32[]{:S(2)}, u32[]{:S(2)}) %collective-permute-start.3) | collective-permute-done | bytes 262176 | tf_op jit(solution)/shard_map/ppermute | solution.py:421
  16.9 0.0 copy-start
  16.9 1.5 %shard_map.100 = (bf16[16,64,128]{2,1,0:T(8,128)(2,1)S(1)}, bf16[320,128]{1,0:T(8,128)(2,1)S(1)}, bf16[320,128]{1,0:T(8,128)(2,1)S(1)}, bf16[320,128]{1,0:T(8,128)(2,1)S(1)}) custom-call(s32[16,128]{1,0:T(8,128)S(1)} %get-tuple-element.27.bases, bf16[1024,128]{1,0:T(8,128)(2,1)S(1)} %collective-permute-done.2.left, ...), custom_call_target="tpu_custom_call" | custom-call | tf_op jit(solution)/shard_map/pallas_call | solution.py:442
  18.4 2.7 %collective-permute-start.10 = (bf16[320,128]{1,0:T(8,128)(2,1)S(1)}, bf16[320,128]{1,0:T(8,128)(2,1)S(1)}, u32[]{:S(2)}, u32[]{:S(2)}) collective-permute-start(bf16[320,128]{1,0:T(8,128)(2,1)S(1)} %get-tuple-element.45), channel_id=1, source_target_pairs={{0,2},{1,3},{2,0},{3,1},{4,6},{5,7},{6,4},{7,5},{8,10},{9,11},{10,... | collective-permute-start | bytes 245768 | tf_op jit(solution)/shard_map/ppermute | solution.py:459
  21.1 1.3 %collective-permute-start.12 = (bf16[320,128]{1,0:T(8,128)(2,1)S(1)}, bf16[320,128]{1,0:T(8,128)(2,1)S(1)}, u32[]{:S(2)}, u32[]{:S(2)}) collective-permute-start(bf16[320,128]{1,0:T(8,128)(2,1)S(1)} %get-tuple-element.47), channel_id=1, source_target_pairs={{0,3},{1,2},{2,1},{3,0},{4,7},{5,6},{6,5},{7,4},{8,11},{9,10},{10,... | collective-permute-start | bytes 245768 | tf_op jit(solution)/shard_map/ppermute | solution.py:459
  22.4 0.2 collective-permute-start.8
  22.6 2.9 %collective-permute-start.11 = (bf16[320,128]{1,0:T(8,128)(2,1)S(1)}, bf16[320,128]{1,0:T(8,128)(2,1)S(1)}, u32[]{:S(2)}, u32[]{:S(2)}) collective-permute-start(bf16[320,128]{1,0:T(8,128)(2,1)S(1)} %get-tuple-element.46), channel_id=1, source_target_pairs={{0,3},{1,2},{2,1},{3,0},{4,7},{5,6},{6,5},{7,4},{8,11},{9,10},{10,... | collective-permute-start | bytes 245768 | tf_op jit(solution)/shard_map/ppermute | solution.py:459
  25.6 0.0 copy-done
  25.6 2.8 %shard_map.101 = (bf16[2048,128]{1,0:T(8,128)(2,1)}, bf16[1024,128]{1,0:T(8,128)(2,1)S(1)}, bf16[384,128]{1,0:T(8,128)(2,1)S(1)}, bf16[384,128]{1,0:T(8,128)(2,1)S(1)}, bf16[384,128]{1,0:T(8,128)(2,1)S(1)}) custom-call(s32[16,128]{1,0:T(8,128)S(1)} %get-tuple-element.27.bases, bf16[128,128]{1,0:T(8,128)(2,1)S(1)} %copy-done, ...), custom_call_target="tpu_custom_call" | custom-call | tf_op jit(solution)/shard_map/pallas_call | solution.py:463
  28.4 0.5 %collective-permute-start.4 = (bf16[384,128]{1,0:T(8,128)(2,1)S(1)}, bf16[384,128]{1,0:T(8,128)(2,1)S(1)}, u32[]{:S(2)}, u32[]{:S(2)}) collective-permute-start(bf16[384,128]{1,0:T(8,128)(2,1)S(1)} %get-tuple-element.38), channel_id=1, source_target_pairs={{0,1},{1,0},{2,3},{3,2},{4,5},{5,4},{6,7},{7,6},{8,9},{9,8},{10,11... | collective-permute-start | bytes 294920 | tf_op jit(solution)/shard_map/ppermute | solution.py:479
  28.9 0.0 collective-permute-done.10.refs_3_
  28.9 1.0 %collective-permute-start.5 = (bf16[384,128]{1,0:T(8,128)(2,1)S(1)}, bf16[384,128]{1,0:T(8,128)(2,1)S(1)}, u32[]{:S(2)}, u32[]{:S(2)}) collective-permute-start(bf16[384,128]{1,0:T(8,128)(2,1)S(1)} %get-tuple-element.39), channel_id=1, source_target_pairs={{0,2},{1,3},{2,0},{3,1},{4,6},{5,7},{6,4},{7,5},{8,10},{9,11},{10,... | collective-permute-start | bytes 294920 | tf_op jit(solution)/shard_map/ppermute | solution.py:479
  29.9 0.0 collective-permute-done.12.refs_5_
  29.9 2.9 %collective-permute-start.6 = (bf16[384,128]{1,0:T(8,128)(2,1)S(1)}, bf16[384,128]{1,0:T(8,128)(2,1)S(1)}, u32[]{:S(2)}, u32[]{:S(2)}) collective-permute-start(bf16[384,128]{1,0:T(8,128)(2,1)S(1)} %get-tuple-element.40), channel_id=1, source_target_pairs={{0,3},{1,2},{2,1},{3,0},{4,7},{5,6},{6,5},{7,4},{8,11},{9,10},{10,... | collective-permute-start | bytes 294920 | tf_op jit(solution)/shard_map/ppermute | solution.py:479
  32.9 0.0 collective-permute-done.8.refs_1_
  32.9 2.0 %collective-permute-start.7 = (bf16[320,128]{1,0:T(8,128)(2,1)S(1)}, bf16[320,128]{1,0:T(8,128)(2,1)S(1)}, u32[]{:S(2)}, u32[]{:S(2)}) collective-permute-start(bf16[320,128]{1,0:T(8,128)(2,1)S(1)} %get-tuple-element.42), channel_id=1, source_target_pairs={{0,1},{1,0},{2,3},{3,2},{4,5},{5,4},{6,7},{7,6},{8,9},{9,8},{10,11... | collective-permute-start | bytes 245768 | tf_op jit(solution)/shard_map/ppermute | solution.py:459
  34.8 0.0 collective-permute-done.11.refs_4_
  34.8 5.4 %collective-permute-start.9 = (bf16[320,128]{1,0:T(8,128)(2,1)S(1)}, bf16[320,128]{1,0:T(8,128)(2,1)S(1)}, u32[]{:S(2)}, u32[]{:S(2)}) collective-permute-start(bf16[320,128]{1,0:T(8,128)(2,1)S(1)} %get-tuple-element.44), channel_id=1, source_target_pairs={{0,2},{1,3},{2,0},{3,1},{4,6},{5,7},{6,4},{7,5},{8,10},{9,11},{10,... | collective-permute-start | bytes 245768 | tf_op jit(solution)/shard_map/ppermute | solution.py:459
  40.2 0.8 %collective-permute-done.7.refs_0_ = bf16[320,128]{1,0:T(8,128)(2,1)S(1)} collective-permute-done((bf16[320,128]{1,0:T(8,128)(2,1)S(1)}, bf16[320,128]{1,0:T(8,128)(2,1)S(1)}, u32[]{:S(2)}, u32[]{:S(2)}) %collective-permute-start.7) | collective-permute-done | bytes 81952 | tf_op jit(solution)/shard_map/ppermute | solution.py:459
  41.0 4.3 %collective-permute-done.9.refs_2_ = bf16[320,128]{1,0:T(8,128)(2,1)S(1)} collective-permute-done((bf16[320,128]{1,0:T(8,128)(2,1)S(1)}, bf16[320,128]{1,0:T(8,128)(2,1)S(1)}, u32[]{:S(2)}, u32[]{:S(2)}) %collective-permute-start.9) | collective-permute-done | bytes 81952 | tf_op jit(solution)/shard_map/ppermute | solution.py:459
  45.4 2.5 %shard_map.102.refs_3_ = bf16[4,1024,128]{2,1,0:T(8,128)(2,1)} custom-call(bf16[128,128]{1,0:T(8,128)(2,1)S(1)} %copy-done, bf16[1024,128]{1,0:T(8,128)(2,1)S(1)} %get-tuple-element.41.mine, bf16[320,128]{1,0:T(8,128)(2,1)S(1)} %collective-permute-done.7.refs_0_, bf16[320,128]{1,0:T(8,128)(2,1)S(1)} %collective-permute-done.8.refs_1_, ...), custom_call_target="tpu_custom_call" | custom-call | tf_op jit(solution)/shard_map/pallas_call | solution.py:481
  47.9 0.0 collective-permute-done.4.refs_0_
  47.9 0.0 collective-permute-done.5.refs_1_
  47.9 0.0 collective-permute-done.6.refs_2_
  47.9 0.7 %shard_map.103 = bf16[4,1024,128]{2,1,0:T(8,128)(2,1)} custom-call(bf16[384,128]{1,0:T(8,128)(2,1)S(1)} %collective-permute-done.4.refs_0_, bf16[384,128]{1,0:T(8,128)(2,1)S(1)} %collective-permute-done.5.refs_1_, bf16[384,128]{1,0:T(8,128)(2,1)S(1)} %collective-permute-done.6.refs_2_, ...), custom_call_target="tpu_custom_call", output_to_operand_aliasing={{}: (3, {})} | custom-call | tf_op jit(solution)/shard_map/pallas_call | solution.py:492
Async XLA Ops:
  2.0 8.5 %collective-permute-start = (bf16[1040,128]{1,0:T(8,128)(2,1)S(1)}, bf16[1040,128]{1,0:T(8,128)(2,1)S(1)}, u32[]{:S(2)}, u32[]{:S(2)}) collective-permute-start(bf16[1040,128]{1,0:T(8,128)(2,1)S(1)} %get-tuple-element.29.high), channel_id=1, source_target_pairs={{0,4},{4,8},{8,12},{12,16},{16,20},{20,24},{24,28},{28,0},{1,5},{5... | collective-permute-start | bytes 798728 | tf_op jit(solution)/shard_map/ppermute | solution.py:420
  2.6 9.7 %collective-permute-start.1 = (bf16[1040,128]{1,0:T(8,128)(2,1)S(1)}, bf16[1040,128]{1,0:T(8,128)(2,1)S(1)}, u32[]{:S(2)}, u32[]{:S(2)}) collective-permute-start(bf16[1040,128]{1,0:T(8,128)(2,1)S(1)} %get-tuple-element.29.high), channel_id=1, source_target_pairs={{4,0},{8,4},{12,8},{16,12},{20,16},{24,20},{28,24},{0,28},{5,1},{9... | collective-permute-start | bytes 798728 | tf_op jit(solution)/shard_map/ppermute | solution.py:421
  5.5 2.8 %copy-start.1 = (f32[32,128]{1,0:T(8,128)S(1)}, f32[32,128]{1,0:T(8,128)}, u32[]{:S(2)}) copy-start(f32[32,128]{1,0:T(8,128)} %rates.3) | copy-start | bytes 49156
  5.5 2.8 %copy-start.2 = (s32[2048]{0:T(1024)S(1)}, s32[2048]{0:T(1024)}, u32[]{:S(2)}) copy-start(s32[2048]{0:T(1024)} %param.12) | copy-start | bytes 24580
  5.7 9.8 %collective-permute-start.2 = (bf16[1024,128]{1,0:T(8,128)(2,1)S(1)}, bf16[1024,128]{1,0:T(8,128)(2,1)S(1)}, u32[]{:S(2)}, u32[]{:S(2)}) collective-permute-start(bf16[1024,128]{1,0:T(8,128)(2,1)S(1)} %shard_map.98.high), channel_id=1, source_target_pairs={{0,4},{4,8},{8,12},{12,16},{16,20},{20,24},{24,28},{28,0},{1,5},{5... | collective-permute-start | bytes 786440 | tf_op jit(solution)/shard_map/ppermute | solution.py:420
  5.7 11.2 %collective-permute-start.3 = (bf16[1024,128]{1,0:T(8,128)(2,1)S(1)}, bf16[1024,128]{1,0:T(8,128)(2,1)S(1)}, u32[]{:S(2)}, u32[]{:S(2)}) collective-permute-start(bf16[1024,128]{1,0:T(8,128)(2,1)S(1)} %shard_map.98.high), channel_id=1, source_target_pairs={{4,0},{8,4},{12,8},{16,12},{20,16},{24,20},{28,24},{0,28},{5,1},{9... | collective-permute-start | bytes 786440 | tf_op jit(solution)/shard_map/ppermute | solution.py:421
  8.4 1.1 %copy-start.3 = (s32[2048,1]{0,1:T(1,128)S(1)}, s32[2048,1]{0,1:T(1,128)}, u32[]{:S(2)}) copy-start(s32[2048,1]{0,1:T(1,128)} %param.13) | copy-start | bytes 24580
  16.9 8.7 %copy-start = (bf16[128,128]{1,0:T(8,128)(2,1)S(1)}, bf16[128,128]{1,0:T(8,128)(2,1)}, u32[]{:S(2)}) copy-start(bf16[128,128]{1,0:T(8,128)(2,1)} %reaction.3) | copy-start | bytes 98308
  18.4 10.5 %collective-permute-start.10 = (bf16[320,128]{1,0:T(8,128)(2,1)S(1)}, bf16[320,128]{1,0:T(8,128)(2,1)S(1)}, u32[]{:S(2)}, u32[]{:S(2)}) collective-permute-start(bf16[320,128]{1,0:T(8,128)(2,1)S(1)} %get-tuple-element.45), channel_id=1, source_target_pairs={{0,2},{1,3},{2,0},{3,1},{4,6},{5,7},{6,4},{7,5},{8,10},{9,11},{10,... | collective-permute-start | bytes 245768 | tf_op jit(solution)/shard_map/ppermute | solution.py:459
  21.1 8.9 %collective-permute-start.12 = (bf16[320,128]{1,0:T(8,128)(2,1)S(1)}, bf16[320,128]{1,0:T(8,128)(2,1)S(1)}, u32[]{:S(2)}, u32[]{:S(2)}) collective-permute-start(bf16[320,128]{1,0:T(8,128)(2,1)S(1)} %get-tuple-element.47), channel_id=1, source_target_pairs={{0,3},{1,2},{2,1},{3,0},{4,7},{5,6},{6,5},{7,4},{8,11},{9,10},{10,... | collective-permute-start | bytes 245768 | tf_op jit(solution)/shard_map/ppermute | solution.py:459
  22.4 10.5 %collective-permute-start.8 = (bf16[320,128]{1,0:T(8,128)(2,1)S(1)}, bf16[320,128]{1,0:T(8,128)(2,1)S(1)}, u32[]{:S(2)}, u32[]{:S(2)}) collective-permute-start(bf16[320,128]{1,0:T(8,128)(2,1)S(1)} %get-tuple-element.43), channel_id=1, source_target_pairs={{0,1},{1,0},{2,3},{3,2},{4,5},{5,4},{6,7},{7,6},{8,9},{9,8},{10,11... | collective-permute-start | bytes 245768 | tf_op jit(solution)/shard_map/ppermute | solution.py:459
  22.6 12.2 %collective-permute-start.11 = (bf16[320,128]{1,0:T(8,128)(2,1)S(1)}, bf16[320,128]{1,0:T(8,128)(2,1)S(1)}, u32[]{:S(2)}, u32[]{:S(2)}) collective-permute-start(bf16[320,128]{1,0:T(8,128)(2,1)S(1)} %get-tuple-element.46), channel_id=1, source_target_pairs={{0,3},{1,2},{2,1},{3,0},{4,7},{5,6},{6,5},{7,4},{8,11},{9,10},{10,... | collective-permute-start | bytes 245768 | tf_op jit(solution)/shard_map/ppermute | solution.py:459
  28.4 19.5 %collective-permute-start.4 = (bf16[384,128]{1,0:T(8,128)(2,1)S(1)}, bf16[384,128]{1,0:T(8,128)(2,1)S(1)}, u32[]{:S(2)}, u32[]{:S(2)}) collective-permute-start(bf16[384,128]{1,0:T(8,128)(2,1)S(1)} %get-tuple-element.38), channel_id=1, source_target_pairs={{0,1},{1,0},{2,3},{3,2},{4,5},{5,4},{6,7},{7,6},{8,9},{9,8},{10,11... | collective-permute-start | bytes 294920 | tf_op jit(solution)/shard_map/ppermute | solution.py:479
  28.9 19.0 %collective-permute-start.5 = (bf16[384,128]{1,0:T(8,128)(2,1)S(1)}, bf16[384,128]{1,0:T(8,128)(2,1)S(1)}, u32[]{:S(2)}, u32[]{:S(2)}) collective-permute-start(bf16[384,128]{1,0:T(8,128)(2,1)S(1)} %get-tuple-element.39), channel_id=1, source_target_pairs={{0,2},{1,3},{2,0},{3,1},{4,6},{5,7},{6,4},{7,5},{8,10},{9,11},{10,... | collective-permute-start | bytes 294920 | tf_op jit(solution)/shard_map/ppermute | solution.py:479
  29.9 18.0 %collective-permute-start.6 = (bf16[384,128]{1,0:T(8,128)(2,1)S(1)}, bf16[384,128]{1,0:T(8,128)(2,1)S(1)}, u32[]{:S(2)}, u32[]{:S(2)}) collective-permute-start(bf16[384,128]{1,0:T(8,128)(2,1)S(1)} %get-tuple-element.40), channel_id=1, source_target_pairs={{0,3},{1,2},{2,1},{3,0},{4,7},{5,6},{6,5},{7,4},{8,11},{9,10},{10,... | collective-permute-start | bytes 294920 | tf_op jit(solution)/shard_map/ppermute | solution.py:479
  32.9 8.2 %collective-permute-start.7 = (bf16[320,128]{1,0:T(8,128)(2,1)S(1)}, bf16[320,128]{1,0:T(8,128)(2,1)S(1)}, u32[]{:S(2)}, u32[]{:S(2)}) collective-permute-start(bf16[320,128]{1,0:T(8,128)(2,1)S(1)} %get-tuple-element.42), channel_id=1, source_target_pairs={{0,1},{1,0},{2,3},{3,2},{4,5},{5,4},{6,7},{7,6},{8,9},{9,8},{10,11... | collective-permute-start | bytes 245768 | tf_op jit(solution)/shard_map/ppermute | solution.py:459
  34.8 10.5 %collective-permute-start.9 = (bf16[320,128]{1,0:T(8,128)(2,1)S(1)}, bf16[320,128]{1,0:T(8,128)(2,1)S(1)}, u32[]{:S(2)}, u32[]{:S(2)}) collective-permute-start(bf16[320,128]{1,0:T(8,128)(2,1)S(1)} %get-tuple-element.44), channel_id=1, source_target_pairs={{0,2},{1,3},{2,0},{3,1},{4,6},{5,7},{6,4},{7,5},{8,10},{9,11},{10,... | collective-permute-start | bytes 245768 | tf_op jit(solution)/shard_map/ppermute | solution.py:459
